TPU v7x, 256 devices: a whole 4x4x8 slice. The times are simulated.
256 devices in a mesh: beads: 64 (over x, y, z_hi, core), waves: 4 (over z_lo).
Axes of the slice: x: 4, y: 4, z: 8 (z_hi: 2, z_lo: 4; z = z_hi * 4 + z_lo), core: 2. Of those that a mesh axis runs over, the one named last changes fastest.
Arguments:
- positions: float32 [3, 32768], P(None, 'beads'), may hold values from 0 to 256
- features: bfloat16 [32768, 256], P(('beads', 'waves')), may hold values from -6 to 6
- cotangent: bfloat16 [32768, 256], P(('beads', 'waves')), may hold values from -6 to 6
- wavevectors: float32 [3, 4096], replicated, may hold values from -0.25 to 0.25
- filter_gain: bfloat16 [4096, 256], P(('beads', 'waves')), may hold values from -6 to 6
Outputs:
- grad_features: bfloat16 [32768, 256], P(('beads', 'waves'))
- grad_positions: float32 [3, 32768], P(None, ('beads', 'waves'))
- grad_filter: float32 [4096, 256], P(('beads', 'waves'))
All inputs are finite; a program needn't handle non-finite values.
Results may differ from a plain program's by a relative error of at most 0.012.
Values may be sent and summed in bfloat16 or wider, within the bound.
No kernel may reach another device: no remote copies, remote signals or barrier semaphores. Data moves between devices by JAX's collectives and lax.ppermute only.
A program may use at most 64 MiB of HBM per device.

v0:
```python
import math

import jax
import jax.numpy as jnp
from jax import lax
from jax.experimental import pallas as pl
from jax.experimental.pallas import tpu as pltpu
from jax.sharding import Mesh
from jax.sharding import PartitionSpec as P


ALL = ("x", "y", "zh", "core", "zl")
Z = ("zh", "zl")
XY = ("x", "y")
BF16 = jnp.bfloat16
F32 = jnp.float32
LANES = 128

SIN_TURN = (6.28318501, -41.3416557, 81.6010056, -76.5497818, 39.536705)


def sin_turn(h):
    s = h * h
    poly = SIN_TURN[-1]
    for c in SIN_TURN[-2::-1]:
        poly = poly * s + c
    return poly * h


def load_kernel(cot, feat, pos, wv, own, pos_near, wv_near, sems):
    width = cot.shape[1]
    copies = [
        pltpu.make_async_copy(cot, own.at[:, :width], sems.at[0]),
        pltpu.make_async_copy(feat, own.at[:, width:], sems.at[1]),
        pltpu.make_async_copy(pos, pos_near, sems.at[2]),
        pltpu.make_async_copy(wv, wv_near, sems.at[3]),
    ]
    for c in copies:
        c.start()
    for c in copies:
        c.wait()


def trig_rows(kcols, pos, cs, zh, zl, first):
    n_xy = cs.shape[1]
    n_z = cs.shape[4] // LANES
    n_zl = n_z // 2
    columns = [
        pl.multiple_of(lax.rem(zh * n_zl + zl + n_z - first - i, n_z) * LANES, LANES)
        for i in range(n_zl)
    ]

    def step(i, carry):
        dc, xy = i // n_xy, lax.rem(i, n_xy)
        cols = kcols[pl.ds(pl.multiple_of(i * 16, 16), 16), :]
        t = cols[:, 0:1] * pos[0:1] + cols[:, 1:2] * pos[1:2] + cols[:, 2:3] * pos[2:3]
        f = t - jnp.round(t)
        cosine = sin_turn(0.25 - jnp.abs(f)).astype(BF16)
        sine = sin_turn(jnp.maximum(jnp.minimum(f, 0.5 - f), -0.5 - f)).astype(BF16)
        for j, column in enumerate(columns):
            part = slice(j * LANES, (j + 1) * LANES)
            cs[dc, xy, 0, :, pl.ds(column, LANES)] = cosine[:, part]
            cs[dc, xy, 1, :, pl.ds(column, LANES)] = sine[:, part]
        return carry

    lax.fori_loop(0, 2 * n_xy, step, 0, unroll=4)


def trig_near_kernel(pos, wv, cs, kvrel, kcols, kvt):
    zh, zl, core = (lax.axis_index(a) for a in ("zh", "zl", "core"))
    n_xy = cs.shape[1]
    n_zl = cs.shape[4] // LANES // 2
    for xy in range(n_xy):
        at = pl.multiple_of((xy * 2 + zh) * LANES, LANES)
        piece = wv[:, pl.ds(at, LANES)]
        piece = jnp.concatenate([piece, jnp.zeros((5, LANES), F32)], 0)
        kvt[xy, :, 0:8] = piece.T
    for dc in range(2):
        at = pl.multiple_of((jnp.bitwise_xor(core, dc) * n_zl + zl) * 16, 16)
        for xy in range(n_xy):
            cols = kvt[xy, pl.ds(at, 16), 0:8]
            rows = slice((dc * n_xy + xy) * 16, (dc * n_xy + xy + 1) * 16)
            hi = cols.astype(BF16)
            lo = (cols - hi.astype(F32)).astype(BF16)
            kvrel[rows, :] = jnp.concatenate([hi, lo], 1)
            kcols[rows, :] = cols * (1.0 / (2.0 * math.pi))
    trig_rows(kcols, pos[...], cs, zh, zl, zh * n_zl)


def trig_far_kernel(pos, kcols, _, cs):
    zh, zl = lax.axis_index("zh"), lax.axis_index("zl")
    n_zl = cs.shape[4] // LANES // 2
    trig_rows(kcols, pos[...], cs, zh, zl, jnp.bitwise_xor(zh, 1) * n_zl)


def joined(pieces):
    return jnp.concatenate([p[:LANES] for p in pieces], 0)


def early_kernel(cs, *refs):
    pieces, out = refs[:-1], refs[-1]
    rows = cs[...].reshape(-1, cs.shape[4])
    n = rows.shape[1] // 2
    rows = jnp.concatenate([rows[:, :n], rows[:, n + LANES :]], 1)
    part = jnp.dot(rows, joined(pieces), preferred_element_type=F32)
    out[...] = part.reshape(out.shape)


def late_kernel(dc, cs, early, block, out):
    rows = cs[dc].reshape(-1, cs.shape[4])
    n = rows.shape[1] // 2
    part = jnp.dot(rows[:, n : n + LANES], block[...], preferred_element_type=F32)
    out[...] = (part.reshape(out.shape) + early[dc]).astype(out.dtype)


def filter_kernel(spec_scale, wave_scale, arrived, gain, out, grad_filter):
    n = arrived.shape[0]
    width = gain.shape[1]
    total = arrived[0].astype(F32)
    for i in range(1, n):
        total = total + arrived[i].astype(F32)
    total = total.reshape(2, 16, 2 * width)
    cot = total[:, :, :width] * wave_scale
    spec = total[:, :, width:] * spec_scale
    g = gain[...].astype(F32)
    grad_filter[...] = cot[0] * spec[0] + cot[1] * spec[1]
    filt = (g[None] * spec * (wave_scale / spec_scale)).astype(BF16)
    dspec = (g[None] * cot).astype(BF16)
    both = jnp.concatenate([filt, dspec], 2).reshape(32, 2 * width)
    for i in range(n):
        out[i] = both


def half_gradients(dc, cs, kvrel, stacked, beads_all):
    n_xy, beads = cs.shape[1], cs.shape[4]
    width = beads_all.shape[1] // 2
    both = stacked[...].reshape(n_xy * 32, 2 * width)
    ab = lax.dot_general(both, beads_all, (((1,), (1,)), ((), ())), preferred_element_type=F32)
    ab = ab.reshape(n_xy, 2, 16, beads)
    d = cs[dc, :, 0].astype(F32) * ab[:, 1] - cs[dc, :, 1].astype(F32) * ab[:, 0]
    d = d.reshape(n_xy * 16, beads).astype(BF16)
    kv = kvrel[dc * n_xy * 16 : (dc + 1) * n_xy * 16, :]
    gp = lax.dot_general(kv, d, (((0,), (0,)), ((), ())), preferred_element_type=F32)
    rows = cs[dc].reshape(n_xy * 32, beads)
    gf = lax.dot_general(
        both[:, width:], rows, (((0,), (0,)), ((), ())), preferred_element_type=F32
    )
    return gf, gp[0:8] + gp[8:16]


def grads_near_kernel(cs, kvrel, stacked, *refs):
    pieces, (gf_out, gp_out) = refs[:-2], refs[-2:]
    beads_all = joined(pieces)
    gf, gp = half_gradients(0, cs, kvrel, stacked, beads_all)
    gf_out[...] = gf
    gp_out[...] = gp


def grads_far_kernel(cs, kvrel, stacked, gf_in, gp_in, *refs):
    pieces, out = refs[:-1], refs[-1]
    beads_all = joined(pieces)
    gf, gp = half_gradients(1, cs, kvrel, stacked, beads_all)
    gf = (gf + gf_in[...]).astype(BF16)
    gp = gp + gp_in[...]
    hi = gp.astype(BF16).astype(F32)
    tail = jnp.concatenate([hi[0:3], (gp - hi)[0:3], jnp.zeros_like(gp[0:2])], 0).astype(BF16)
    n_z = out.shape[0]
    width = gf.shape[0]
    here = lax.axis_index(Z)
    for shift in range(n_z):
        at = slice(shift * LANES, (shift + 1) * LANES)
        to = lax.rem(here + n_z - shift, n_z)
        out[to, 0:width, :] = gf[:, at]
        out[to, width : width + 8, :] = tail[:, at]


def total_kernel(spec_scale, arrived, grad_filter, gf_out, gp_out, filter_out):
    total = arrived[0].astype(F32)
    for i in range(1, arrived.shape[0]):
        total = total + arrived[i].astype(F32)
    total = total * spec_scale
    width = gf_out.shape[1]
    gf_out[...] = total[:width].T.astype(BF16)
    gp_out[...] = total[width : width + 3] + total[width + 3 : width + 6]
    filter_out[...] = grad_filter[...]


def call(kernel, out_shape, n_in, scratch=(), aliases=None, space=pltpu.VMEM):
    specs = [pl.BlockSpec(memory_space=space)] * n_in
    outs = jax.tree.map(lambda _: pl.BlockSpec(memory_space=pltpu.VMEM), out_shape)
    return pl.pallas_call(
        kernel,
        out_shape=out_shape,
        in_specs=specs,
        out_specs=outs,
        scratch_shapes=scratch,
        input_output_aliases=aliases or {},
        compiler_params=pltpu.CompilerParams(vmem_limit_bytes=16 << 20),
    )


def shape(dims, dtype):
    return jax.ShapeDtypeStruct(dims, dtype)


def body(positions, features, cotangent, wavevectors, filter_gain):
    n_z = lax.axis_size(Z)
    n_xy = lax.axis_size(XY)
    beads_dev, width = features.shape
    beads_grp = beads_dev * n_z
    n_beads = beads_grp * n_xy * 2
    spec_scale = 1.0 / math.sqrt(n_beads)
    wave_scale = 1.0 / math.sqrt(wavevectors.shape[1])

    def along_z(a, k):
        return lax.ppermute(a, Z, [(i, (i + k) % n_z) for i in range(n_z)])

    def across(a):
        return lax.ppermute(a, "core", [(0, 1), (1, 0)])

    inputs = (cotangent, features, positions, wavevectors)
    inputs = [pltpu.with_memory_space_constraint(a, pltpu.HBM) for a in inputs]
    own, pos_near, wv_near = call(
        load_kernel,
        (
            shape((beads_dev, 2 * width), BF16),
            shape(positions.shape, F32),
            shape(wavevectors.shape, F32),
        ),
        4,
        scratch=[pltpu.SemaphoreType.DMA((4,))],
        space=pltpu.HBM,
    )(*inputs)
    pieces = {0: own, 2: along_z(own, 2), 6: along_z(own, -2)}

    n_rows = 2 * n_xy * 16
    cs_shape = shape((2, n_xy, 2, 16, beads_grp), BF16)
    trig = call(
        trig_near_kernel,
        (cs_shape, shape((n_rows, 16), BF16), shape((n_rows, 8), F32)),
        2,
        scratch=[pltpu.VMEM((n_xy, LANES, 8), F32)],
    )(pos_near, wv_near)
    own, trig, pos_near = lax.optimization_barrier((own, trig, pos_near))
    pieces[1], pieces[7] = along_z(own, 1), along_z(own, -1)
    turns = [2 if i % (n_z // 2) < n_z // 4 else -2 for i in range(n_z)]
    pos_far = lax.ppermute(pos_near, Z, [((i - turns[i]) % n_z, i) for i in range(n_z)])
    pieces[2], pieces[6], trig = lax.optimization_barrier((pieces[2], pieces[6], trig))
    pieces[3], pieces[5] = along_z(pieces[2], 1), along_z(pieces[6], -1)
    cs = call(trig_far_kernel, cs_shape, 3, aliases={2: 0})(pos_far, trig[2], trig[0])
    kvrel = trig[1]
    pieces[3], pieces[5], cs = lax.optimization_barrier((pieces[3], pieces[5], cs))
    onward = jnp.where(lax.axis_index("core") == 0, pieces[3], pieces[5])
    n_zl = lax.axis_size("zl")

    def at(z, core):
        return (z // n_zl * 2 + core) * n_zl + z % n_zl

    pairs = [(at(z, c), at((z + 1 - 2 * c) % n_z, c)) for z in range(n_z) for c in range(2)]
    pieces[4] = lax.ppermute(onward, ("zh", "core", "zl"), pairs)
    blocks = [pieces[k] for k in range(n_z)]
    near_blocks = [blocks[k] for k in range(n_z) if k != n_z // 2]
    early = call(
        early_kernel, shape((2, n_xy, 32, 2 * width), F32), 1 + len(near_blocks)
    )(cs, *near_blocks)

    def spectra(dc, dtype):
        return call(
            lambda *refs: late_kernel(dc, *refs),
            shape((n_xy, 32, 2 * width), dtype),
            3,
        )(cs, early, pieces[4])

    theirs = across(spectra(1, BF16))
    mine = (spectra(0, F32) + theirs.astype(F32)).astype(BF16)
    arrived = lax.all_to_all(mine, XY, 0, 0, tiled=True)
    copies, grad_filter = call(
        lambda *refs: filter_kernel(spec_scale, wave_scale, *refs),
        (shape((n_xy, 32, 2 * width), BF16), shape((16, width), F32)),
        2,
    )(arrived, filter_gain)
    near = lax.all_to_all(copies, XY, 0, 0, tiled=True)
    far = across(near)
    gf, gp = call(
        grads_near_kernel,
        (shape((width, beads_grp), F32), shape((8, beads_grp), F32)),
        3 + len(blocks),
    )(cs, kvrel, near, *blocks)
    parts = call(
        grads_far_kernel,
        shape((n_z, width + 8, beads_dev), BF16),
        5 + len(blocks),
    )(cs, kvrel, far, gf, gp, *blocks)
    outs = (
        shape((beads_dev, width), BF16),
        shape((3, beads_dev), F32),
        shape((16, width), F32),
    )
    return call(lambda *refs: total_kernel(spec_scale, *refs), outs, 2)(
        lax.all_to_all(parts, Z, 0, 0, tiled=True), grad_filter
    )


def solution(mesh):
    torus = Mesh(mesh.devices.reshape(4, 4, 2, 2, mesh.shape["waves"]), ALL)
    beads = ("x", "y", "zh", "core")
    return jax.shard_map(
        body,
        mesh=torus,
        in_specs=(P(None, beads), P(ALL, None), P(ALL, None), P(), P(ALL, None)),
        out_specs=(P(ALL, None), P(None, ALL), P(ALL, None)),
        check_vma=False,
    )
```

profile of v0, /device:TPU:1, one launch (start us, length us, event | category | flops | bytes accessed | tf_op | source)
XLA Modules:
  0.0 95.4 jit_solution(205560583114561887)
XLA Ops:
  0.6 1.0 %shard_map.76 = (bf16[128,512]{1,0:T(8,128)(2,1)S(1)}, f32[3,512]{1,0:T(4,128)S(1)}, f32[3,4096]{1,0:T(4,128)S(1)}) custom-call(bf16[128,256]{1,0:T(8,128)(2,1)} %cot.1, bf16[128,256]{1,0:T(8,128)(2,1)} %feat.1, f32[3,512]{1,0:T(4,128)} %pos.1, f32[3,4096]{1,0:T(4,128)} %wv.1), custom_call_target="tpu_custom_call" | custom-call | tf_op jit(solution)/shard_map/pallas_call | solution.py:223
  1.6 6.9 %collective-permute-start.1 = (bf16[128,512]{1,0:T(8,128)(2,1)S(1)}, bf16[128,512]{1,0:T(8,128)(2,1)S(1)}, u32[]{:S(2)}, u32[]{:S(2)}) collective-permute-start(bf16[128,512]{1,0:T(8,128)(2,1)S(1)} %get-tuple-element.42.refs_0_), channel_id=1, source_target_pairs={{0,10},{1,11},{2,0},{3,1},{8,2},{9,3},{10,8},{11,9},{4,14},{5,15},... | collective-permute-start | bytes 393224 | tf_op jit(solution)/shard_map/ppermute | solution.py:216
  8.5 0.0 collective-permute-start
  8.5 2.3 %shard_map.77 = (bf16[2,16,2,16,1024]{4,3,2,1,0:T(8,128)(2,1)S(1)}, bf16[512,16]{1,0:T(8,128)(2,1)S(1)}, f32[512,8]{1,0:T(8,128)S(1)}) custom-call(f32[3,512]{1,0:T(4,128)S(1)} %get-tuple-element.37.pos, f32[3,4096]{1,0:T(4,128)S(1)} %get-tuple-element.28.wv), custom_call_target="tpu_custom_call" | custom-call | tf_op jit(solution)/shard_map/pallas_call | solution.py:238
  10.8 0.7 collective-permute-done.1.refs_5_.refs_6_
  11.5 4.4 %collective-permute-done.refs_2_ = bf16[128,512]{1,0:T(8,128)(2,1)S(1)} collective-permute-done((bf16[128,512]{1,0:T(8,128)(2,1)S(1)}, bf16[128,512]{1,0:T(8,128)(2,1)S(1)}, u32[]{:S(2)}, u32[]{:S(2)}) %collective-permute-start) | collective-permute-done | bytes 131104 | tf_op jit(solution)/shard_map/ppermute | solution.py:216
  15.8 3.1 %collective-permute-start.2 = (bf16[128,512]{1,0:T(8,128)(2,1)S(1)}, bf16[128,512]{1,0:T(8,128)(2,1)S(1)}, u32[]{:S(2)}, u32[]{:S(2)}) collective-permute-start(bf16[128,512]{1,0:T(8,128)(2,1)S(1)} %collective-permute-done.refs_2_), channel_id=1, source_target_pairs={{0,1},{1,2},{2,3},{3,8},{8,9},{9,10},{10,11},{11,0},{4,5},{5,6},{6... | collective-permute-start | bytes 393224 | tf_op jit(solution)/shard_map/ppermute | solution.py:216
  18.9 0.0 collective-permute-start.3
  18.9 0.8 collective-permute-start.4
  19.7 3.1 %collective-permute-start.6 = (bf16[128,512]{1,0:T(8,128)(2,1)S(1)}, bf16[128,512]{1,0:T(8,128)(2,1)S(1)}, u32[]{:S(2)}, u32[]{:S(2)}) collective-permute-start(bf16[128,512]{1,0:T(8,128)(2,1)S(1)} %get-tuple-element.42.refs_0_), channel_id=1, source_target_pairs={{0,11},{1,0},{2,1},{3,2},{8,3},{9,8},{10,9},{11,10},{4,15},{5,4},{... | collective-permute-start | bytes 393224 | tf_op jit(solution)/shard_map/ppermute | solution.py:216
  22.8 0.0 collective-permute-start.5
  22.8 0.9 collective-permute-done.4.pos
  23.6 1.8 %shard_map.78.cs.refs_0_ = bf16[2,16,2,16,1024]{4,3,2,1,0:T(8,128)(2,1)S(1)} custom-call(f32[3,512]{1,0:T(4,128)S(1)} %collective-permute-done.4.pos, f32[512,8]{1,0:T(8,128)S(1)} %get-tuple-element.38.kcols, bf16[2,16,2,16,1024]{4,3,2,1,0:T(8,128)(2,1)S(1)} %get-tuple-element.39._), custom_call_target="tpu_custom_call", output_to_operand_aliasing={{}: (2, {})} | custom-call | tf_op jit(solution)/shard_map/pallas_call | solution.py:250
  25.4 0.0 collective-permute-done.2.refs_3_
  25.4 0.0 collective-permute-done.3.refs_4_.refs_5_
  25.5 1.9 %collective-permute-start.7 = (bf16[128,512]{1,0:T(8,128)(2,1)S(1)}, bf16[128,512]{1,0:T(8,128)(2,1)S(1)}, u32[]{:S(2)}, u32[]{:S(2)}) collective-permute-start(bf16[128,512]{1,0:T(8,128)(2,1)S(1)} %broadcast_select_fusion), channel_id=1, source_target_pairs={{0,1},{4,15},{1,2},{5,4},{2,3},{6,5},{3,8},{7,6},{8,9},{12,7},{9,1... | collective-permute-start | bytes 393224 | tf_op jit(solution)/shard_map/ppermute | solution.py:260
  27.4 0.0 collective-permute-done.6.refs_6_.refs_7_
  27.4 0.5 collective-permute-done.5.refs_1_
  27.9 1.2 %shard_map.79.refs_1_ = f32[2,16,32,512]{3,2,1,0:T(8,128)S(1)} custom-call(bf16[2,16,2,16,1024]{4,3,2,1,0:T(8,128)(2,1)S(1)} %shard_map.78.cs.refs_0_, bf16[128,512]{1,0:T(8,128)(2,1)S(1)} %get-tuple-element.42.refs_0_, bf16[128,512]{1,0:T(8,128)(2,1)S(1)} %collective-permute-done.5.refs_1_, bf16[128,512]{1,0:T(8,128)(2,1)S(1)} %collective-permute-done.refs_2_, ...), custom_call_target="tpu_custom_call" | custom-call | tf_op jit(solution)/shard_map/pallas_call | solution.py:263
  29.1 0.6 collective-permute-done.7.refs_2_.refs_4_
  29.7 0.3 shard_map.81
  29.9 6.5 %collective-permute-start.8 = (bf16[16,32,512]{2,1,0:T(8,128)(2,1)S(1)}, bf16[16,32,512]{2,1,0:T(8,128)(2,1)S(1)}, u32[]{:S(2)}, u32[]{:S(2)}) collective-permute-start(bf16[16,32,512]{2,1,0:T(8,128)(2,1)S(1)} %shard_map.81), channel_id=1, source_target_pairs={{0,4},{4,0},{1,5},{5,1},{2,6},{6,2},{3,7},{7,3},{8,12},{12,8},{9,1... | collective-permute-start | bytes 1572872 | tf_op jit(solution)/shard_map/ppermute | solution.py:219
  36.5 0.3 shard_map.80
  36.8 0.0 copy-start
  36.8 1.2 %collective-permute-done.8 = bf16[16,32,512]{2,1,0:T(8,128)(2,1)S(1)} collective-permute-done((bf16[16,32,512]{2,1,0:T(8,128)(2,1)S(1)}, bf16[16,32,512]{2,1,0:T(8,128)(2,1)S(1)}, u32[]{:S(2)}, u32[]{:S(2)}) %collective-permute-start.8) | collective-permute-done | bytes 524320 | tf_op jit(solution)/shard_map/ppermute | solution.py:219
  38.0 0.2 add_convert_fusion
  38.2 16.9 %all_to_all.15.refs_0_ = bf16[16,32,512]{2,1,0:T(8,128)(2,1)S(1)} all-to-all(bf16[16,32,512]{2,1,0:T(8,128)(2,1)S(1)} %add_convert_fusion), channel_id=1, replica_groups=mesh['x'=4,'y'=4,'zh'=2,'core'=2,'zl'=4] {'x','y'}, dimensions={0} | all-to-all | bytes 1048576 | tf_op jit(solution)/shard_map/all_to_all | solution.py:276
  55.1 0.0 copy-done
  55.1 0.1 shard_map.82
  55.3 12.7 %all_to_all.16.stacked = bf16[16,32,512]{2,1,0:T(8,128)(2,1)S(1)} all-to-all(bf16[16,32,512]{2,1,0:T(8,128)(2,1)S(1)} %get-tuple-element.45), channel_id=1, replica_groups=mesh['x'=4,'y'=4,'zh'=2,'core'=2,'zl'=4] {'x','y'}, dimensions={0} | all-to-all | bytes 1048576 | tf_op jit(solution)/shard_map/all_to_all | solution.py:282
  68.0 3.2 %collective-permute-start.9 = (bf16[16,32,512]{2,1,0:T(8,128)(2,1)S(1)}, bf16[16,32,512]{2,1,0:T(8,128)(2,1)S(1)}, u32[]{:S(2)}, u32[]{:S(2)}) collective-permute-start(bf16[16,32,512]{2,1,0:T(8,128)(2,1)S(1)} %all_to_all.16.stacked), channel_id=1, source_target_pairs={{0,4},{4,0},{1,5},{5,1},{2,6},{6,2},{3,7},{7,3},{8,12},{12,8},{9,1... | collective-permute-start | bytes 1572872 | tf_op jit(solution)/shard_map/ppermute | solution.py:219
  71.2 1.2 %shard_map.83 = (f32[256,1024]{1,0:T(8,128)S(1)}, f32[8,1024]{1,0:T(8,128)S(1)}) custom-call(bf16[2,16,2,16,1024]{4,3,2,1,0:T(8,128)(2,1)S(1)} %shard_map.78.cs.refs_0_, bf16[512,16]{1,0:T(8,128)(2,1)S(1)} %get-tuple-element.41.kvrel, bf16[16,32,512]{2,1,0:T(8,128)(2,1)S(1)} %all_to_all.16.stacked, bf16[128,512]{1,0:T(8,128)(2,1)S(1)} %get-tuple-element.42.refs_0_, ...), custom_call_target="tpu_custom_call" | custom-call | tf_op jit(solution)/shard_map/pallas_call | solution.py:284
  72.4 0.4 collective-permute-done.9.stacked
  72.8 1.2 %shard_map.84 = bf16[8,264,128]{2,1,0:T(8,128)(2,1)S(1)} custom-call(bf16[2,16,2,16,1024]{4,3,2,1,0:T(8,128)(2,1)S(1)} %shard_map.78.cs.refs_0_, bf16[512,16]{1,0:T(8,128)(2,1)S(1)} %get-tuple-element.41.kvrel, bf16[16,32,512]{2,1,0:T(8,128)(2,1)S(1)} %collective-permute-done.9.stacked, f32[256,1024]{1,0:T(8,128)S(1)} %get-tuple-element.46.gf_in, ...), custom_call_target="tpu_custom_call" | custom-call | tf_op jit(solution)/shard_map/pallas_call | solution.py:289
  74.0 20.7 %all_to_all.17.refs_0_ = bf16[8,264,128]{2,1,0:T(8,128)(2,1)S(1)} all-to-all(bf16[8,264,128]{2,1,0:T(8,128)(2,1)S(1)} %shard_map.84), channel_id=1, replica_groups=mesh['x'=4,'y'=4,'zh'=2,'core'=2,'zl'=4] {'zh','zl'}, dimensions={0} | all-to-all | bytes 1081344 | tf_op jit(solution)/shard_map/all_to_all | solution.py:300
  94.6 0.8 shard_map.85
  (1 shorter events, 0.0 us)
Async XLA Ops:
  1.6 9.9 %collective-permute-start.1 = (bf16[128,512]{1,0:T(8,128)(2,1)S(1)}, bf16[128,512]{1,0:T(8,128)(2,1)S(1)}, u32[]{:S(2)}, u32[]{:S(2)}) collective-permute-start(bf16[128,512]{1,0:T(8,128)(2,1)S(1)} %get-tuple-element.42.refs_0_), channel_id=1, source_target_pairs={{0,10},{1,11},{2,0},{3,1},{8,2},{9,3},{10,8},{11,9},{4,14},{5,15},... | collective-permute-start | bytes 393224 | tf_op jit(solution)/shard_map/ppermute | solution.py:216
  8.5 7.3 %collective-permute-start = (bf16[128,512]{1,0:T(8,128)(2,1)S(1)}, bf16[128,512]{1,0:T(8,128)(2,1)S(1)}, u32[]{:S(2)}, u32[]{:S(2)}) collective-permute-start(bf16[128,512]{1,0:T(8,128)(2,1)S(1)} %get-tuple-element.42.refs_0_), channel_id=1, source_target_pairs={{0,2},{1,3},{2,8},{3,9},{8,10},{9,11},{10,0},{11,1},{4,6},{5,7},{6... | collective-permute-start | bytes 393224 | tf_op jit(solution)/shard_map/ppermute | solution.py:216
  15.8 9.6 %collective-permute-start.2 = (bf16[128,512]{1,0:T(8,128)(2,1)S(1)}, bf16[128,512]{1,0:T(8,128)(2,1)S(1)}, u32[]{:S(2)}, u32[]{:S(2)}) collective-permute-start(bf16[128,512]{1,0:T(8,128)(2,1)S(1)} %collective-permute-done.refs_2_), channel_id=1, source_target_pairs={{0,1},{1,2},{2,3},{3,8},{8,9},{9,10},{10,11},{11,0},{4,5},{5,6},{6... | collective-permute-start | bytes 393224 | tf_op jit(solution)/shard_map/ppermute | solution.py:216
  18.9 6.5 %collective-permute-start.3 = (bf16[128,512]{1,0:T(8,128)(2,1)S(1)}, bf16[128,512]{1,0:T(8,128)(2,1)S(1)}, u32[]{:S(2)}, u32[]{:S(2)}) collective-permute-start(bf16[128,512]{1,0:T(8,128)(2,1)S(1)} %collective-permute-done.1.refs_5_.refs_6_), channel_id=1, source_target_pairs={{0,11},{1,0},{2,1},{3,2},{8,3},{9,8},{10,9},{11,10},{4,15},{5,4},{... | collective-permute-start | bytes 393224 | tf_op jit(solution)/shard_map/ppermute | solution.py:216
  18.9 4.7 %collective-permute-start.4 = (f32[3,512]{1,0:T(4,128)S(1)}, f32[3,512]{1,0:T(4,128)S(1)}, u32[]{:S(2)}, u32[]{:S(2)}) collective-permute-start(f32[3,512]{1,0:T(4,128)S(1)} %get-tuple-element.37.pos), channel_id=1, source_target_pairs={{10,0},{11,1},{8,2},{9,3},{2,8},{3,9},{0,10},{1,11},{14,4},{15,5},... | collective-permute-start | bytes 18440 | tf_op jit(solution)/shard_map/ppermute | solution.py:247
  19.7 7.7 %collective-permute-start.6 = (bf16[128,512]{1,0:T(8,128)(2,1)S(1)}, bf16[128,512]{1,0:T(8,128)(2,1)S(1)}, u32[]{:S(2)}, u32[]{:S(2)}) collective-permute-start(bf16[128,512]{1,0:T(8,128)(2,1)S(1)} %get-tuple-element.42.refs_0_), channel_id=1, source_target_pairs={{0,11},{1,0},{2,1},{3,2},{8,3},{9,8},{10,9},{11,10},{4,15},{5,4},{... | collective-permute-start | bytes 393224 | tf_op jit(solution)/shard_map/ppermute | solution.py:216
  22.8 5.1 %collective-permute-start.5 = (bf16[128,512]{1,0:T(8,128)(2,1)S(1)}, bf16[128,512]{1,0:T(8,128)(2,1)S(1)}, u32[]{:S(2)}, u32[]{:S(2)}) collective-permute-start(bf16[128,512]{1,0:T(8,128)(2,1)S(1)} %get-tuple-element.42.refs_0_), channel_id=1, source_target_pairs={{0,1},{1,2},{2,3},{3,8},{8,9},{9,10},{10,11},{11,0},{4,5},{5,6},{6... | collective-permute-start | bytes 393224 | tf_op jit(solution)/shard_map/ppermute | solution.py:216
  25.5 4.2 %collective-permute-start.7 = (bf16[128,512]{1,0:T(8,128)(2,1)S(1)}, bf16[128,512]{1,0:T(8,128)(2,1)S(1)}, u32[]{:S(2)}, u32[]{:S(2)}) collective-permute-start(bf16[128,512]{1,0:T(8,128)(2,1)S(1)} %broadcast_select_fusion), channel_id=1, source_target_pairs={{0,1},{4,15},{1,2},{5,4},{2,3},{6,5},{3,8},{7,6},{8,9},{12,7},{9,1... | collective-permute-start | bytes 393224 | tf_op jit(solution)/shard_map/ppermute | solution.py:260
  29.9 8.1 %collective-permute-start.8 = (bf16[16,32,512]{2,1,0:T(8,128)(2,1)S(1)}, bf16[16,32,512]{2,1,0:T(8,128)(2,1)S(1)}, u32[]{:S(2)}, u32[]{:S(2)}) collective-permute-start(bf16[16,32,512]{2,1,0:T(8,128)(2,1)S(1)} %shard_map.81), channel_id=1, source_target_pairs={{0,4},{4,0},{1,5},{5,1},{2,6},{6,2},{3,7},{7,3},{8,12},{12,8},{9,1... | collective-permute-start | bytes 1572872 | tf_op jit(solution)/shard_map/ppermute | solution.py:219
  36.8 18.4 %copy-start = (bf16[16,256]{1,0:T(8,128)(2,1)S(1)}, bf16[16,256]{1,0:T(8,128)(2,1)}, u32[]{:S(2)}) copy-start(bf16[16,256]{1,0:T(8,128)(2,1)} %refs_1_.1) | copy-start | bytes 24580
  68.0 4.8 %collective-permute-start.9 = (bf16[16,32,512]{2,1,0:T(8,128)(2,1)S(1)}, bf16[16,32,512]{2,1,0:T(8,128)(2,1)S(1)}, u32[]{:S(2)}, u32[]{:S(2)}) collective-permute-start(bf16[16,32,512]{2,1,0:T(8,128)(2,1)S(1)} %all_to_all.16.stacked), channel_id=1, source_target_pairs={{0,4},{4,0},{1,5},{5,1},{2,6},{6,2},{3,7},{7,3},{8,12},{12,8},{9,1... | collective-permute-start | bytes 1572872 | tf_op jit(solution)/shard_map/ppermute | solution.py:219
where the time goes:
time: 95.6 us; the launch traced here: 95.4 us
  blocking collectives  50.3 us (53%)
  starting transfers between devices  25.5 us (27%)
  Pallas kernels  10.1 us (11%)
  waiting for transfers between devices  8.56 us (9%)
    all_to_all x1, blocking collectives, body(): lax.all_to_all(parts, Z, 0, 0, tiled=True)  20.7 us
    all_to_all x1, blocking collectives, body(): arrived = lax.all_to_all(mine, XY, 0, 0, tiled=True)  16.9 us
    ppermute x6, starting transfers between devices, along_z(): return lax.ppermute(a, Z, [(i, (i + k) % n_z) for i in range(n_z)])  13 us
    all_to_all x1, blocking collectives, body(): near = lax.all_to_all(copies, XY, 0, 0, tiled=True)  12.7 us
    ppermute x2, starting transfers between devices, across(): return lax.ppermute(a, 'core', [(0, 1), (1, 0)])  9.78 us
    ppermute x6, waiting for transfers between devices, along_z(): return lax.ppermute(a, Z, [(i, (i + k) % n_z) for i in range(n_z)])  5.55 us
    pallas_call x1, Pallas kernels, body(): call(trig_near_kernel, (cs_shape, shape((n_rows, 16), BF16), shape((n_row...  2.26 us
  transfers between devices with their start and end apart: 10, of which 7 were waited for; matrix products, arithmetic and copies ran while one was open for 0% of the time, Pallas kernels for 7%

commit v1 on v0

--- a/solution.py
+++ b/solution.py
@@ -246,19 +246,20 @@
     turns = [2 if i % (n_z // 2) < n_z // 4 else -2 for i in range(n_z)]
     pos_far = lax.ppermute(pos_near, Z, [((i - turns[i]) % n_z, i) for i in range(n_z)])
     pieces[2], pieces[6], trig = lax.optimization_barrier((pieces[2], pieces[6], trig))
-    pieces[3], pieces[5] = along_z(pieces[2], 1), along_z(pieces[6], -1)
+    ahead, behind = pieces[2], pieces[6]
+    onward = jnp.where(lax.axis_index("core") == 0, ahead, behind)
+    n_zl = lax.axis_size("zl")
+
+    def at(z, core):
+        return (z // n_zl * 2 + core) * n_zl + z % n_zl
+
+    pairs = [(at(z, c), at((z + 2 - 4 * c) % n_z, c)) for z in range(n_z) for c in range(2)]
+    pieces[4] = lax.ppermute(onward, ("zh", "core", "zl"), pairs)
+    pieces[3], pieces[5] = along_z(ahead, 1), along_z(behind, -1)
+    blocks = [pieces[k] for k in range(n_z)]
     cs = call(trig_far_kernel, cs_shape, 3, aliases={2: 0})(pos_far, trig[2], trig[0])
     kvrel = trig[1]
-    pieces[3], pieces[5], cs = lax.optimization_barrier((pieces[3], pieces[5], cs))
-    onward = jnp.where(lax.axis_index("core") == 0, pieces[3], pieces[5])
-    n_zl = lax.axis_size("zl")
-
-    def at(z, core):
-        return (z // n_zl * 2 + core) * n_zl + z % n_zl
-
-    pairs = [(at(z, c), at((z + 1 - 2 * c) % n_z, c)) for z in range(n_z) for c in range(2)]
-    pieces[4] = lax.ppermute(onward, ("zh", "core", "zl"), pairs)
-    blocks = [pieces[k] for k in range(n_z)]
+
     near_blocks = [blocks[k] for k in range(n_z) if k != n_z // 2]
     early = call(
         early_kernel, shape((2, n_xy, 32, 2 * width), F32), 1 + len(near_blocks)

time: 95.6 us -> 90 us (0.941)
  the two profiles are of different devices: /device:TPU:1 before, /device:TPU:8 now
where the time goes in v1:
time: 90 us; the launch traced here: 88.4 us
  blocking collectives  52.3 us (58%)
  starting transfers between devices  15.9 us (18%)
  Pallas kernels  10.1 us (11%)
  waiting for transfers between devices  9.04 us (10%)
    all_to_all x1, blocking collectives, body(): lax.all_to_all(parts, Z, 0, 0, tiled=True)  20.8 us
    all_to_all x1, blocking collectives, body(): arrived = lax.all_to_all(mine, XY, 0, 0, tiled=True)  17.6 us
    all_to_all x1, blocking collectives, body(): near = lax.all_to_all(copies, XY, 0, 0, tiled=True)  13.9 us
    ppermute x6, starting transfers between devices, along_z(): return lax.ppermute(a, Z, [(i, (i + k) % n_z) for i in range(n_z)])  13.4 us
    ppermute x6, waiting for transfers between devices, along_z(): return lax.ppermute(a, Z, [(i, (i + k) % n_z) for i in range(n_z)])  4.64 us
    ppermute x1, starting transfers between devices, body(): lax.ppermute(pos_near, Z, [((i - turns[i]) % n_z, i) for i in range(n_z)])  2.47 us
    ppermute x2, waiting for transfers between devices, across(): return lax.ppermute(a, 'core', [(0, 1), (1, 0)])  2.32 us
    pallas_call x1, Pallas kernels, body(): call(trig_near_kernel, (cs_shape, shape((n_rows, 16), BF16), shape((n_row...  2.26 us
  transfers between devices with their start and end apart: 10, of which 7 were waited for; matrix products, arithmetic and copies ran while one was open for 0% of the time, Pallas kernels for 8%

profile of v1, /device:TPU:8, one launch (start us, length us, event | category | flops | bytes accessed | tf_op | source)
XLA Modules:
  0.0 88.4 jit_solution(5385831335914817090)
XLA Ops:
  0.6 1.0 %shard_map.76 = (bf16[128,512]{1,0:T(8,128)(2,1)S(1)}, f32[3,512]{1,0:T(4,128)S(1)}, f32[3,4096]{1,0:T(4,128)S(1)}) custom-call(bf16[128,256]{1,0:T(8,128)(2,1)} %cot.1, bf16[128,256]{1,0:T(8,128)(2,1)} %feat.1, f32[3,512]{1,0:T(4,128)} %pos.1, f32[3,4096]{1,0:T(4,128)} %wv.1), custom_call_target="tpu_custom_call" | custom-call | tf_op jit(solution)/shard_map/pallas_call | solution.py:223
  1.6 6.4 %collective-permute-start.2 = (bf16[128,512]{1,0:T(8,128)(2,1)S(1)}, bf16[128,512]{1,0:T(8,128)(2,1)S(1)}, u32[]{:S(2)}, u32[]{:S(2)}) collective-permute-start(bf16[128,512]{1,0:T(8,128)(2,1)S(1)} %get-tuple-element.36.refs_0_), channel_id=1, source_target_pairs={{0,10},{1,11},{2,0},{3,1},{8,2},{9,3},{10,8},{11,9},{4,14},{5,15},... | collective-permute-start | bytes 393224 | tf_op jit(solution)/shard_map/ppermute | solution.py:216
  8.0 0.0 collective-permute-start.1
  8.0 2.3 %shard_map.77 = (bf16[2,16,2,16,1024]{4,3,2,1,0:T(8,128)(2,1)S(1)}, bf16[512,16]{1,0:T(8,128)(2,1)S(1)}, f32[512,8]{1,0:T(8,128)S(1)}) custom-call(f32[3,512]{1,0:T(4,128)S(1)} %get-tuple-element.29.pos, f32[3,4096]{1,0:T(4,128)S(1)} %get-tuple-element.25.wv), custom_call_target="tpu_custom_call" | custom-call | tf_op jit(solution)/shard_map/pallas_call | solution.py:238
  10.2 3.8 %collective-permute-start.6 = (bf16[128,512]{1,0:T(8,128)(2,1)S(1)}, bf16[128,512]{1,0:T(8,128)(2,1)S(1)}, u32[]{:S(2)}, u32[]{:S(2)}) collective-permute-start(bf16[128,512]{1,0:T(8,128)(2,1)S(1)} %get-tuple-element.36.refs_0_), channel_id=1, source_target_pairs={{0,11},{1,0},{2,1},{3,2},{8,3},{9,8},{10,9},{11,10},{4,15},{5,4},{... | collective-permute-start | bytes 393224 | tf_op jit(solution)/shard_map/ppermute | solution.py:216
  14.0 0.0 collective-permute-start.3
  14.0 2.5 %collective-permute-start = (f32[3,512]{1,0:T(4,128)S(1)}, f32[3,512]{1,0:T(4,128)S(1)}, u32[]{:S(2)}, u32[]{:S(2)}) collective-permute-start(f32[3,512]{1,0:T(4,128)S(1)} %get-tuple-element.29.pos), channel_id=1, source_target_pairs={{10,0},{11,1},{8,2},{9,3},{2,8},{3,9},{0,10},{1,11},{14,4},{15,5},... | collective-permute-start | bytes 18440 | tf_op jit(solution)/shard_map/ppermute | solution.py:247
  16.5 0.0 collective-permute-done.2.refs_5_.refs_6_
  16.5 0.7 collective-permute-done.1.refs_2_
  17.1 2.2 %collective-permute-start.4 = (bf16[128,512]{1,0:T(8,128)(2,1)S(1)}, bf16[128,512]{1,0:T(8,128)(2,1)S(1)}, u32[]{:S(2)}, u32[]{:S(2)}) collective-permute-start(bf16[128,512]{1,0:T(8,128)(2,1)S(1)} %collective-permute-done.1.refs_2_), channel_id=1, source_target_pairs={{0,1},{1,2},{2,3},{3,8},{8,9},{9,10},{10,11},{11,0},{4,5},{5,6},{6... | collective-permute-start | bytes 393224 | tf_op jit(solution)/shard_map/ppermute | solution.py:216
  19.4 1.0 %collective-permute-start.5 = (bf16[128,512]{1,0:T(8,128)(2,1)S(1)}, bf16[128,512]{1,0:T(8,128)(2,1)S(1)}, u32[]{:S(2)}, u32[]{:S(2)}) collective-permute-start(bf16[128,512]{1,0:T(8,128)(2,1)S(1)} %collective-permute-done.2.refs_5_.refs_6_), channel_id=1, source_target_pairs={{0,11},{1,0},{2,1},{3,2},{8,3},{9,8},{10,9},{11,10},{4,15},{5,4},{... | collective-permute-start | bytes 393224 | tf_op jit(solution)/shard_map/ppermute | solution.py:216
  20.4 0.6 collective-permute-done.pos
  21.0 0.0 collective-permute-start.7
  21.0 1.8 %shard_map.78.cs.refs_0_ = bf16[2,16,2,16,1024]{4,3,2,1,0:T(8,128)(2,1)S(1)} custom-call(f32[3,512]{1,0:T(4,128)S(1)} %collective-permute-done.pos, f32[512,8]{1,0:T(8,128)S(1)} %get-tuple-element.33.kcols, bf16[2,16,2,16,1024]{4,3,2,1,0:T(8,128)(2,1)S(1)} %get-tuple-element.34._), custom_call_target="tpu_custom_call", output_to_operand_aliasing={{}: (2, {})} | custom-call | tf_op jit(solution)/shard_map/pallas_call | solution.py:260
  22.8 0.0 collective-permute-done.6.refs_6_.refs_7_
  22.8 0.0 collective-permute-done.3.refs_1_
  22.8 0.5 collective-permute-done.4.refs_3_
  23.4 3.4 %collective-permute-done.5.refs_4_.refs_5_ = bf16[128,512]{1,0:T(8,128)(2,1)S(1)} collective-permute-done((bf16[128,512]{1,0:T(8,128)(2,1)S(1)}, bf16[128,512]{1,0:T(8,128)(2,1)S(1)}, u32[]{:S(2)}, u32[]{:S(2)}) %collective-permute-start.5) | collective-permute-done | bytes 131104 | tf_op jit(solution)/shard_map/ppermute | solution.py:216
  26.8 1.2 %shard_map.79.refs_1_ = f32[2,16,32,512]{3,2,1,0:T(8,128)S(1)} custom-call(bf16[2,16,2,16,1024]{4,3,2,1,0:T(8,128)(2,1)S(1)} %shard_map.78.cs.refs_0_, bf16[128,512]{1,0:T(8,128)(2,1)S(1)} %get-tuple-element.36.refs_0_, bf16[128,512]{1,0:T(8,128)(2,1)S(1)} %collective-permute-done.3.refs_1_, bf16[128,512]{1,0:T(8,128)(2,1)S(1)} %collective-permute-done.1.refs_2_, ...), custom_call_target="tpu_custom_call" | custom-call | tf_op jit(solution)/shard_map/pallas_call | solution.py:264
  28.1 1.5 %collective-permute-done.7.refs_2_.refs_4_ = bf16[128,512]{1,0:T(8,128)(2,1)S(1)} collective-permute-done((bf16[128,512]{1,0:T(8,128)(2,1)S(1)}, bf16[128,512]{1,0:T(8,128)(2,1)S(1)}, u32[]{:S(2)}, u32[]{:S(2)}) %collective-permute-start.7) | collective-permute-done | bytes 131104 | tf_op jit(solution)/shard_map/ppermute | solution.py:257
  29.5 0.3 shard_map.81
  29.8 0.1 collective-permute-start.8
  29.9 0.3 shard_map.80
  30.2 0.0 copy-start
  30.2 1.6 %collective-permute-done.8 = bf16[16,32,512]{2,1,0:T(8,128)(2,1)S(1)} collective-permute-done((bf16[16,32,512]{2,1,0:T(8,128)(2,1)S(1)}, bf16[16,32,512]{2,1,0:T(8,128)(2,1)S(1)}, u32[]{:S(2)}, u32[]{:S(2)}) %collective-permute-start.8) | collective-permute-done | bytes 524320 | tf_op jit(solution)/shard_map/ppermute | solution.py:219
  31.8 0.2 add_convert_fusion
  32.0 17.6 %all_to_all.15.refs_0_ = bf16[16,32,512]{2,1,0:T(8,128)(2,1)S(1)} all-to-all(bf16[16,32,512]{2,1,0:T(8,128)(2,1)S(1)} %add_convert_fusion), channel_id=1, replica_groups=mesh['x'=4,'y'=4,'zh'=2,'core'=2,'zl'=4] {'x','y'}, dimensions={0} | all-to-all | bytes 1048576 | tf_op jit(solution)/shard_map/all_to_all | solution.py:277
  49.6 0.0 copy-done
  49.6 0.1 shard_map.82
  49.7 13.9 %all_to_all.16.stacked = bf16[16,32,512]{2,1,0:T(8,128)(2,1)S(1)} all-to-all(bf16[16,32,512]{2,1,0:T(8,128)(2,1)S(1)} %get-tuple-element.39), channel_id=1, replica_groups=mesh['x'=4,'y'=4,'zh'=2,'core'=2,'zl'=4] {'x','y'}, dimensions={0} | all-to-all | bytes 1048576 | tf_op jit(solution)/shard_map/all_to_all | solution.py:283
  63.6 0.0 collective-permute-start.9
  63.6 1.2 %shard_map.83 = (f32[256,1024]{1,0:T(8,128)S(1)}, f32[8,1024]{1,0:T(8,128)S(1)}) custom-call(bf16[2,16,2,16,1024]{4,3,2,1,0:T(8,128)(2,1)S(1)} %shard_map.78.cs.refs_0_, bf16[512,16]{1,0:T(8,128)(2,1)S(1)} %get-tuple-element.35.kvrel, bf16[16,32,512]{2,1,0:T(8,128)(2,1)S(1)} %all_to_all.16.stacked, bf16[128,512]{1,0:T(8,128)(2,1)S(1)} %get-tuple-element.36.refs_0_, ...), custom_call_target="tpu_custom_call" | custom-call | tf_op jit(solution)/shard_map/pallas_call | solution.py:285
  64.8 0.7 collective-permute-done.9.stacked
  65.6 1.2 %shard_map.84 = bf16[8,264,128]{2,1,0:T(8,128)(2,1)S(1)} custom-call(bf16[2,16,2,16,1024]{4,3,2,1,0:T(8,128)(2,1)S(1)} %shard_map.78.cs.refs_0_, bf16[512,16]{1,0:T(8,128)(2,1)S(1)} %get-tuple-element.35.kvrel, bf16[16,32,512]{2,1,0:T(8,128)(2,1)S(1)} %collective-permute-done.9.stacked, f32[256,1024]{1,0:T(8,128)S(1)} %get-tuple-element.40.gf_in, ...), custom_call_target="tpu_custom_call" | custom-call | tf_op jit(solution)/shard_map/pallas_call | solution.py:290
  66.8 20.8 %all_to_all.17.refs_0_ = bf16[8,264,128]{2,1,0:T(8,128)(2,1)S(1)} all-to-all(bf16[8,264,128]{2,1,0:T(8,128)(2,1)S(1)} %shard_map.84), channel_id=1, replica_groups=mesh['x'=4,'y'=4,'zh'=2,'core'=2,'zl'=4] {'zh','zl'}, dimensions={0} | all-to-all | bytes 1081344 | tf_op jit(solution)/shard_map/all_to_all | solution.py:301
  87.6 0.8 shard_map.85
  (1 shorter events, 0.0 us)
Async XLA Ops:
  1.6 14.9 %collective-permute-start.2 = (bf16[128,512]{1,0:T(8,128)(2,1)S(1)}, bf16[128,512]{1,0:T(8,128)(2,1)S(1)}, u32[]{:S(2)}, u32[]{:S(2)}) collective-permute-start(bf16[128,512]{1,0:T(8,128)(2,1)S(1)} %get-tuple-element.36.refs_0_), channel_id=1, source_target_pairs={{0,10},{1,11},{2,0},{3,1},{8,2},{9,3},{10,8},{11,9},{4,14},{5,15},... | collective-permute-start | bytes 393224 | tf_op jit(solution)/shard_map/ppermute | solution.py:216
  8.0 9.2 %collective-permute-start.1 = (bf16[128,512]{1,0:T(8,128)(2,1)S(1)}, bf16[128,512]{1,0:T(8,128)(2,1)S(1)}, u32[]{:S(2)}, u32[]{:S(2)}) collective-permute-start(bf16[128,512]{1,0:T(8,128)(2,1)S(1)} %get-tuple-element.36.refs_0_), channel_id=1, source_target_pairs={{0,2},{1,3},{2,8},{3,9},{8,10},{9,11},{10,0},{11,1},{4,6},{5,7},{6... | collective-permute-start | bytes 393224 | tf_op jit(solution)/shard_map/ppermute | solution.py:216
  10.2 12.6 %collective-permute-start.6 = (bf16[128,512]{1,0:T(8,128)(2,1)S(1)}, bf16[128,512]{1,0:T(8,128)(2,1)S(1)}, u32[]{:S(2)}, u32[]{:S(2)}) collective-permute-start(bf16[128,512]{1,0:T(8,128)(2,1)S(1)} %get-tuple-element.36.refs_0_), channel_id=1, source_target_pairs={{0,11},{1,0},{2,1},{3,2},{8,3},{9,8},{10,9},{11,10},{4,15},{5,4},{... | collective-permute-start | bytes 393224 | tf_op jit(solution)/shard_map/ppermute | solution.py:216
  14.0 8.8 %collective-permute-start.3 = (bf16[128,512]{1,0:T(8,128)(2,1)S(1)}, bf16[128,512]{1,0:T(8,128)(2,1)S(1)}, u32[]{:S(2)}, u32[]{:S(2)}) collective-permute-start(bf16[128,512]{1,0:T(8,128)(2,1)S(1)} %get-tuple-element.36.refs_0_), channel_id=1, source_target_pairs={{0,1},{1,2},{2,3},{3,8},{8,9},{9,10},{10,11},{11,0},{4,5},{5,6},{6... | collective-permute-start | bytes 393224 | tf_op jit(solution)/shard_map/ppermute | solution.py:216
  14.0 7.0 %collective-permute-start = (f32[3,512]{1,0:T(4,128)S(1)}, f32[3,512]{1,0:T(4,128)S(1)}, u32[]{:S(2)}, u32[]{:S(2)}) collective-permute-start(f32[3,512]{1,0:T(4,128)S(1)} %get-tuple-element.29.pos), channel_id=1, source_target_pairs={{10,0},{11,1},{8,2},{9,3},{2,8},{3,9},{0,10},{1,11},{14,4},{15,5},... | collective-permute-start | bytes 18440 | tf_op jit(solution)/shard_map/ppermute | solution.py:247
  17.1 6.2 %collective-permute-start.4 = (bf16[128,512]{1,0:T(8,128)(2,1)S(1)}, bf16[128,512]{1,0:T(8,128)(2,1)S(1)}, u32[]{:S(2)}, u32[]{:S(2)}) collective-permute-start(bf16[128,512]{1,0:T(8,128)(2,1)S(1)} %collective-permute-done.1.refs_2_), channel_id=1, source_target_pairs={{0,1},{1,2},{2,3},{3,8},{8,9},{9,10},{10,11},{11,0},{4,5},{5,6},{6... | collective-permute-start | bytes 393224 | tf_op jit(solution)/shard_map/ppermute | solution.py:216
  19.4 7.4 %collective-permute-start.5 = (bf16[128,512]{1,0:T(8,128)(2,1)S(1)}, bf16[128,512]{1,0:T(8,128)(2,1)S(1)}, u32[]{:S(2)}, u32[]{:S(2)}) collective-permute-start(bf16[128,512]{1,0:T(8,128)(2,1)S(1)} %collective-permute-done.2.refs_5_.refs_6_), channel_id=1, source_target_pairs={{0,11},{1,0},{2,1},{3,2},{8,3},{9,8},{10,9},{11,10},{4,15},{5,4},{... | collective-permute-start | bytes 393224 | tf_op jit(solution)/shard_map/ppermute | solution.py:216
  21.0 8.5 %collective-permute-start.7 = (bf16[128,512]{1,0:T(8,128)(2,1)S(1)}, bf16[128,512]{1,0:T(8,128)(2,1)S(1)}, u32[]{:S(2)}, u32[]{:S(2)}) collective-permute-start(bf16[128,512]{1,0:T(8,128)(2,1)S(1)} %broadcast_select_fusion), channel_id=1, source_target_pairs={{0,2},{4,14},{1,3},{5,15},{2,8},{6,4},{3,9},{7,5},{8,10},{12,6},{9... | collective-permute-start | bytes 393224 | tf_op jit(solution)/shard_map/ppermute | solution.py:257
  29.8 2.0 %collective-permute-start.8 = (bf16[16,32,512]{2,1,0:T(8,128)(2,1)S(1)}, bf16[16,32,512]{2,1,0:T(8,128)(2,1)S(1)}, u32[]{:S(2)}, u32[]{:S(2)}) collective-permute-start(bf16[16,32,512]{2,1,0:T(8,128)(2,1)S(1)} %shard_map.81), channel_id=1, source_target_pairs={{0,4},{4,0},{1,5},{5,1},{2,6},{6,2},{3,7},{7,3},{8,12},{12,8},{9,1... | collective-permute-start | bytes 1572872 | tf_op jit(solution)/shard_map/ppermute | solution.py:219
  30.2 19.4 %copy-start = (bf16[16,256]{1,0:T(8,128)(2,1)S(1)}, bf16[16,256]{1,0:T(8,128)(2,1)}, u32[]{:S(2)}) copy-start(bf16[16,256]{1,0:T(8,128)(2,1)} %refs_1_.1) | copy-start | bytes 24580
  63.6 1.9 %collective-permute-start.9 = (bf16[16,32,512]{2,1,0:T(8,128)(2,1)S(1)}, bf16[16,32,512]{2,1,0:T(8,128)(2,1)S(1)}, u32[]{:S(2)}, u32[]{:S(2)}) collective-permute-start(bf16[16,32,512]{2,1,0:T(8,128)(2,1)S(1)} %all_to_all.16.stacked), channel_id=1, source_target_pairs={{0,4},{4,0},{1,5},{5,1},{2,6},{6,2},{3,7},{7,3},{8,12},{12,8},{9,1... | collective-permute-start | bytes 1572872 | tf_op jit(solution)/shard_map/ppermute | solution.py:219

commit v2 on v1

--- a/solution.py
+++ b/solution.py
@@ -100,16 +100,17 @@
 def early_kernel(cs, *refs):
     pieces, out = refs[:-1], refs[-1]
     rows = cs[...].reshape(-1, cs.shape[4])
-    n = rows.shape[1] // 2
-    rows = jnp.concatenate([rows[:, :n], rows[:, n + LANES :]], 1)
-    part = jnp.dot(rows, joined(pieces), preferred_element_type=F32)
+    n, m = 3 * LANES, rows.shape[1] - 3 * LANES
+    parts = [rows[:, :n], rows[:, n + LANES : m], rows[:, m + LANES :]]
+    part = jnp.dot(jnp.concatenate(parts, 1), joined(pieces), preferred_element_type=F32)
     out[...] = part.reshape(out.shape)
 
 
-def late_kernel(dc, cs, early, block, out):
+def late_kernel(dc, cs, early, ahead, behind, out):
     rows = cs[dc].reshape(-1, cs.shape[4])
-    n = rows.shape[1] // 2
-    part = jnp.dot(rows[:, n : n + LANES], block[...], preferred_element_type=F32)
+    n, m = 3 * LANES, rows.shape[1] - 3 * LANES
+    rows = jnp.concatenate([rows[:, n : n + LANES], rows[:, m : m + LANES]], 1)
+    part = jnp.dot(rows, joined([ahead, behind]), preferred_element_type=F32)
     out[...] = (part.reshape(out.shape) + early[dc]).astype(out.dtype)
 
 
@@ -247,30 +248,39 @@
     pos_far = lax.ppermute(pos_near, Z, [((i - turns[i]) % n_z, i) for i in range(n_z)])
     pieces[2], pieces[6], trig = lax.optimization_barrier((pieces[2], pieces[6], trig))
     ahead, behind = pieces[2], pieces[6]
-    onward = jnp.where(lax.axis_index("core") == 0, ahead, behind)
+    first = lax.axis_index("core") == 0
+    onward, other = jnp.where(first, ahead, behind), jnp.where(first, behind, ahead)
     n_zl = lax.axis_size("zl")
 
     def at(z, core):
         return (z // n_zl * 2 + core) * n_zl + z % n_zl
 
-    pairs = [(at(z, c), at((z + 2 - 4 * c) % n_z, c)) for z in range(n_z) for c in range(2)]
-    pieces[4] = lax.ppermute(onward, ("zh", "core", "zl"), pairs)
-    pieces[3], pieces[5] = along_z(ahead, 1), along_z(behind, -1)
-    blocks = [pieces[k] for k in range(n_z)]
+    def by_core(a, k):
+        pairs = [(at(z, c), at((z + k - 2 * k * c) % n_z, c)) for z in range(n_z) for c in range(2)]
+        return lax.ppermute(a, ("zh", "core", "zl"), pairs)
+
+    pieces[4] = by_core(onward, 2)
+    crossed = by_core(other, -1)
+    straight = by_core(onward, 1)
     cs = call(trig_far_kernel, cs_shape, 3, aliases={2: 0})(pos_far, trig[2], trig[0])
     kvrel = trig[1]
 
-    near_blocks = [blocks[k] for k in range(n_z) if k != n_z // 2]
+    near_blocks = [pieces[k] for k in (0, 1, 2, 4, 6, 7)]
     early = call(
         early_kernel, shape((2, n_xy, 32, 2 * width), F32), 1 + len(near_blocks)
     )(cs, *near_blocks)
+    early, straight, crossed = lax.optimization_barrier((early, straight, crossed))
+    pieces[3] = jnp.where(first, straight, crossed)
+    pieces[5] = jnp.where(first, crossed, straight)
+    late_blocks = [pieces[3], pieces[5]]
+    blocks = [pieces[k] for k in range(n_z)]
 
     def spectra(dc, dtype):
         return call(
             lambda *refs: late_kernel(dc, *refs),
             shape((n_xy, 32, 2 * width), dtype),
-            3,
-        )(cs, early, pieces[4])
+            2 + len(late_blocks),
+        )(cs, early, *late_blocks)
 
     theirs = across(spectra(1, BF16))
     mine = (spectra(0, F32) + theirs.astype(F32)).astype(BF16)

time: 90 us -> 88.8 us (0.987)
  waiting for transfers between devices: 9.04 us -> 6.34 us
  starting transfers between devices: 15.9 us -> 17.7 us
    ppermute x1 -> x3, starting transfers between devices: 0.01 us -> 4.98 us  [by_core(): return lax.ppermute(a, ('zh', 'core', 'zl'), pairs)]
    ppermute x6 -> x4, waiting for transfers between devices: 4.64 us -> 0.67 us  [along_z(): return lax.ppermute(a, Z, [(i, (i + k) % n_z) for i in range(n_z)])]
    ppermute x6 -> x4, starting transfers between devices: 13.4 us -> 10.1 us  [along_z(): return lax.ppermute(a, Z, [(i, (i + k) % n_z) for i in range(n_z)])]
    ppermute x1 -> x3, waiting for transfers between devices: 1.48 us -> 3.36 us  [by_core(): return lax.ppermute(a, ('zh', 'core', 'zl'), pairs)]
  transfers between devices with their start and end apart: 10 -> 10, of which waited for: 7 -> 5; matrix products, arithmetic and copies ran while one was open for 0% -> 0% of each run, Pallas kernels for 8% -> 7%
where the time goes in v2:
time: 88.8 us; the launch traced here: 87.2 us
  blocking collectives  52.3 us (59%)
  starting transfers between devices  17.7 us (20%)
  Pallas kernels  9.87 us (11%)
  waiting for transfers between devices  6.34 us (7%)
    all_to_all x1, blocking collectives, body(): lax.all_to_all(parts, Z, 0, 0, tiled=True)  20.8 us
    all_to_all x1, blocking collectives, body(): arrived = lax.all_to_all(mine, XY, 0, 0, tiled=True)  17.6 us
    all_to_all x1, blocking collectives, body(): near = lax.all_to_all(copies, XY, 0, 0, tiled=True)  13.9 us
    ppermute x4, starting transfers between devices, along_z(): return lax.ppermute(a, Z, [(i, (i + k) % n_z) for i in range(n_z)])  10.1 us
    ppermute x3, starting transfers between devices, by_core(): return lax.ppermute(a, ('zh', 'core', 'zl'), pairs)  4.98 us
    ppermute x3, waiting for transfers between devices, by_core(): return lax.ppermute(a, ('zh', 'core', 'zl'), pairs)  3.36 us
    ppermute x1, starting transfers between devices, body(): lax.ppermute(pos_near, Z, [((i - turns[i]) % n_z, i) for i in range(n_z)])  2.47 us
    ppermute x2, waiting for transfers between devices, across(): return lax.ppermute(a, 'core', [(0, 1), (1, 0)])  2.31 us
  transfers between devices with their start and end apart: 10, of which 5 were waited for; matrix products, arithmetic and copies ran while one was open for 0% of the time, Pallas kernels for 7%

profile of v2, /device:TPU:8, one launch (start us, length us, event | category | flops | bytes accessed | tf_op | source)
XLA Modules:
  0.0 87.2 jit_solution(5667578499620212192)
XLA Ops:
  0.6 1.0 %shard_map.76 = (bf16[128,512]{1,0:T(8,128)(2,1)S(1)}, f32[3,512]{1,0:T(4,128)S(1)}, f32[3,4096]{1,0:T(4,128)S(1)}) custom-call(bf16[128,256]{1,0:T(8,128)(2,1)} %cot.1, bf16[128,256]{1,0:T(8,128)(2,1)} %feat.1, f32[3,512]{1,0:T(4,128)} %pos.1, f32[3,4096]{1,0:T(4,128)} %wv.1), custom_call_target="tpu_custom_call" | custom-call | tf_op jit(solution)/shard_map/pallas_call | solution.py:224
  1.6 6.4 %collective-permute-start.2 = (bf16[128,512]{1,0:T(8,128)(2,1)S(1)}, bf16[128,512]{1,0:T(8,128)(2,1)S(1)}, u32[]{:S(2)}, u32[]{:S(2)}) collective-permute-start(bf16[128,512]{1,0:T(8,128)(2,1)S(1)} %get-tuple-element.39.refs_0_), channel_id=1, source_target_pairs={{0,10},{1,11},{2,0},{3,1},{8,2},{9,3},{10,8},{11,9},{4,14},{5,15},... | collective-permute-start | bytes 393224 | tf_op jit(solution)/shard_map/ppermute | solution.py:217
  8.0 0.0 collective-permute-start.1
  8.0 2.3 %shard_map.77 = (bf16[2,16,2,16,1024]{4,3,2,1,0:T(8,128)(2,1)S(1)}, bf16[512,16]{1,0:T(8,128)(2,1)S(1)}, f32[512,8]{1,0:T(8,128)S(1)}) custom-call(f32[3,512]{1,0:T(4,128)S(1)} %get-tuple-element.32.pos, f32[3,4096]{1,0:T(4,128)S(1)} %get-tuple-element.28.wv), custom_call_target="tpu_custom_call" | custom-call | tf_op jit(solution)/shard_map/pallas_call | solution.py:239
  10.2 3.8 %collective-permute-start.5 = (bf16[128,512]{1,0:T(8,128)(2,1)S(1)}, bf16[128,512]{1,0:T(8,128)(2,1)S(1)}, u32[]{:S(2)}, u32[]{:S(2)}) collective-permute-start(bf16[128,512]{1,0:T(8,128)(2,1)S(1)} %get-tuple-element.39.refs_0_), channel_id=1, source_target_pairs={{0,11},{1,0},{2,1},{3,2},{8,3},{9,8},{10,9},{11,10},{4,15},{5,4},{... | collective-permute-start | bytes 393224 | tf_op jit(solution)/shard_map/ppermute | solution.py:217
  14.0 0.0 collective-permute-start.3
  14.0 2.5 %collective-permute-start = (f32[3,512]{1,0:T(4,128)S(1)}, f32[3,512]{1,0:T(4,128)S(1)}, u32[]{:S(2)}, u32[]{:S(2)}) collective-permute-start(f32[3,512]{1,0:T(4,128)S(1)} %get-tuple-element.32.pos), channel_id=1, source_target_pairs={{10,0},{11,1},{8,2},{9,3},{2,8},{3,9},{0,10},{1,11},{14,4},{15,5},... | collective-permute-start | bytes 18440 | tf_op jit(solution)/shard_map/ppermute | solution.py:248
  16.5 0.0 collective-permute-done.2.refs_4_.refs_6_
  16.5 0.7 collective-permute-done.1.refs_2_
  17.2 0.1 collective-permute-start.4
  17.3 4.9 %collective-permute-start.7 = (bf16[128,512]{1,0:T(8,128)(2,1)S(1)}, bf16[128,512]{1,0:T(8,128)(2,1)S(1)}, u32[]{:S(2)}, u32[]{:S(2)}) collective-permute-start(bf16[128,512]{1,0:T(8,128)(2,1)S(1)} %get-tuple-element.51), channel_id=1, source_target_pairs={{0,11},{4,5},{1,0},{5,6},{2,1},{6,7},{3,2},{7,12},{8,3},{12,13},{9... | collective-permute-start | bytes 393224 | tf_op jit(solution)/shard_map/ppermute | solution.py:260
  22.2 0.0 collective-permute-done.pos
  22.2 0.0 collective-permute-start.6
  22.2 1.8 %shard_map.78.cs.refs_0_ = bf16[2,16,2,16,1024]{4,3,2,1,0:T(8,128)(2,1)S(1)} custom-call(f32[3,512]{1,0:T(4,128)S(1)} %collective-permute-done.pos, f32[512,8]{1,0:T(8,128)S(1)} %get-tuple-element.36.kcols, bf16[2,16,2,16,1024]{4,3,2,1,0:T(8,128)(2,1)S(1)} %get-tuple-element.37._), custom_call_target="tpu_custom_call", output_to_operand_aliasing={{}: (2, {})} | custom-call | tf_op jit(solution)/shard_map/pallas_call | solution.py:265
  24.0 0.0 collective-permute-done.5.refs_5_.refs_7_
  24.0 0.0 collective-permute-done.3.refs_1_
  24.0 1.4 %collective-permute-done.4.refs_3_.refs_4_ = bf16[128,512]{1,0:T(8,128)(2,1)S(1)} collective-permute-done((bf16[128,512]{1,0:T(8,128)(2,1)S(1)}, bf16[128,512]{1,0:T(8,128)(2,1)S(1)}, u32[]{:S(2)}, u32[]{:S(2)}) %collective-permute-start.4) | collective-permute-done | bytes 131104 | tf_op jit(solution)/shard_map/ppermute | solution.py:260
  25.4 1.0 %shard_map.79.refs_1_ = f32[2,16,32,512]{3,2,1,0:T(8,128)S(1)} custom-call(bf16[2,16,2,16,1024]{4,3,2,1,0:T(8,128)(2,1)S(1)} %shard_map.78.cs.refs_0_, bf16[128,512]{1,0:T(8,128)(2,1)S(1)} %get-tuple-element.39.refs_0_, bf16[128,512]{1,0:T(8,128)(2,1)S(1)} %collective-permute-done.3.refs_1_, bf16[128,512]{1,0:T(8,128)(2,1)S(1)} %collective-permute-done.1.refs_2_, ...), custom_call_target="tpu_custom_call" | custom-call | tf_op jit(solution)/shard_map/pallas_call | solution.py:269
  26.3 0.0 collective-permute-done.7
  26.4 2.0 %collective-permute-done.6 = bf16[128,512]{1,0:T(8,128)(2,1)S(1)} collective-permute-done((bf16[128,512]{1,0:T(8,128)(2,1)S(1)}, bf16[128,512]{1,0:T(8,128)(2,1)S(1)}, u32[]{:S(2)}, u32[]{:S(2)}) %collective-permute-start.6) | collective-permute-done | bytes 131104 | tf_op jit(solution)/shard_map/ppermute | solution.py:260
  28.4 0.3 shard_map.81
  28.7 0.1 collective-permute-start.8
  28.8 0.3 shard_map.80
  29.1 0.0 copy-start
  29.1 1.6 %collective-permute-done.8 = bf16[16,32,512]{2,1,0:T(8,128)(2,1)S(1)} collective-permute-done((bf16[16,32,512]{2,1,0:T(8,128)(2,1)S(1)}, bf16[16,32,512]{2,1,0:T(8,128)(2,1)S(1)}, u32[]{:S(2)}, u32[]{:S(2)}) %collective-permute-start.8) | collective-permute-done | bytes 524320 | tf_op jit(solution)/shard_map/ppermute | solution.py:220
  30.7 0.2 add_convert_fusion
  30.8 17.6 %all_to_all.15.refs_0_ = bf16[16,32,512]{2,1,0:T(8,128)(2,1)S(1)} all-to-all(bf16[16,32,512]{2,1,0:T(8,128)(2,1)S(1)} %add_convert_fusion), channel_id=1, replica_groups=mesh['x'=4,'y'=4,'zh'=2,'core'=2,'zl'=4] {'x','y'}, dimensions={0} | all-to-all | bytes 1048576 | tf_op jit(solution)/shard_map/all_to_all | solution.py:287
  48.4 0.0 copy-done
  48.4 0.1 shard_map.82
  48.6 13.9 %all_to_all.16.stacked = bf16[16,32,512]{2,1,0:T(8,128)(2,1)S(1)} all-to-all(bf16[16,32,512]{2,1,0:T(8,128)(2,1)S(1)} %get-tuple-element.45), channel_id=1, replica_groups=mesh['x'=4,'y'=4,'zh'=2,'core'=2,'zl'=4] {'x','y'}, dimensions={0} | all-to-all | bytes 1048576 | tf_op jit(solution)/shard_map/all_to_all | solution.py:293
  62.5 0.0 collective-permute-start.9
  62.5 1.2 %shard_map.83 = (f32[256,1024]{1,0:T(8,128)S(1)}, f32[8,1024]{1,0:T(8,128)S(1)}) custom-call(bf16[2,16,2,16,1024]{4,3,2,1,0:T(8,128)(2,1)S(1)} %shard_map.78.cs.refs_0_, bf16[512,16]{1,0:T(8,128)(2,1)S(1)} %get-tuple-element.38.kvrel, bf16[16,32,512]{2,1,0:T(8,128)(2,1)S(1)} %all_to_all.16.stacked, bf16[128,512]{1,0:T(8,128)(2,1)S(1)} %get-tuple-element.39.refs_0_, ...), custom_call_target="tpu_custom_call" | custom-call | tf_op jit(solution)/shard_map/pallas_call | solution.py:295
  63.7 0.7 collective-permute-done.9.stacked
  64.4 1.2 %shard_map.84 = bf16[8,264,128]{2,1,0:T(8,128)(2,1)S(1)} custom-call(bf16[2,16,2,16,1024]{4,3,2,1,0:T(8,128)(2,1)S(1)} %shard_map.78.cs.refs_0_, bf16[512,16]{1,0:T(8,128)(2,1)S(1)} %get-tuple-element.38.kvrel, bf16[16,32,512]{2,1,0:T(8,128)(2,1)S(1)} %collective-permute-done.9.stacked, f32[256,1024]{1,0:T(8,128)S(1)} %get-tuple-element.46.gf_in, ...), custom_call_target="tpu_custom_call" | custom-call | tf_op jit(solution)/shard_map/pallas_call | solution.py:300
  65.6 20.8 %all_to_all.17.refs_0_ = bf16[8,264,128]{2,1,0:T(8,128)(2,1)S(1)} all-to-all(bf16[8,264,128]{2,1,0:T(8,128)(2,1)S(1)} %shard_map.84), channel_id=1, replica_groups=mesh['x'=4,'y'=4,'zh'=2,'core'=2,'zl'=4] {'zh','zl'}, dimensions={0} | all-to-all | bytes 1081344 | tf_op jit(solution)/shard_map/all_to_all | solution.py:311
  86.4 0.8 shard_map.85
  (2 shorter events, 0.0 us)
Async XLA Ops:
  1.6 14.9 %collective-permute-start.2 = (bf16[128,512]{1,0:T(8,128)(2,1)S(1)}, bf16[128,512]{1,0:T(8,128)(2,1)S(1)}, u32[]{:S(2)}, u32[]{:S(2)}) collective-permute-start(bf16[128,512]{1,0:T(8,128)(2,1)S(1)} %get-tuple-element.39.refs_0_), channel_id=1, source_target_pairs={{0,10},{1,11},{2,0},{3,1},{8,2},{9,3},{10,8},{11,9},{4,14},{5,15},... | collective-permute-start | bytes 393224 | tf_op jit(solution)/shard_map/ppermute | solution.py:217
  8.0 9.2 %collective-permute-start.1 = (bf16[128,512]{1,0:T(8,128)(2,1)S(1)}, bf16[128,512]{1,0:T(8,128)(2,1)S(1)}, u32[]{:S(2)}, u32[]{:S(2)}) collective-permute-start(bf16[128,512]{1,0:T(8,128)(2,1)S(1)} %get-tuple-element.39.refs_0_), channel_id=1, source_target_pairs={{0,2},{1,3},{2,8},{3,9},{8,10},{9,11},{10,0},{11,1},{4,6},{5,7},{6... | collective-permute-start | bytes 393224 | tf_op jit(solution)/shard_map/ppermute | solution.py:217
  10.2 13.7 %collective-permute-start.5 = (bf16[128,512]{1,0:T(8,128)(2,1)S(1)}, bf16[128,512]{1,0:T(8,128)(2,1)S(1)}, u32[]{:S(2)}, u32[]{:S(2)}) collective-permute-start(bf16[128,512]{1,0:T(8,128)(2,1)S(1)} %get-tuple-element.39.refs_0_), channel_id=1, source_target_pairs={{0,11},{1,0},{2,1},{3,2},{8,3},{9,8},{10,9},{11,10},{4,15},{5,4},{... | collective-permute-start | bytes 393224 | tf_op jit(solution)/shard_map/ppermute | solution.py:217
  14.0 10.0 %collective-permute-start.3 = (bf16[128,512]{1,0:T(8,128)(2,1)S(1)}, bf16[128,512]{1,0:T(8,128)(2,1)S(1)}, u32[]{:S(2)}, u32[]{:S(2)}) collective-permute-start(bf16[128,512]{1,0:T(8,128)(2,1)S(1)} %get-tuple-element.39.refs_0_), channel_id=1, source_target_pairs={{0,1},{1,2},{2,3},{3,8},{8,9},{9,10},{10,11},{11,0},{4,5},{5,6},{6... | collective-permute-start | bytes 393224 | tf_op jit(solution)/shard_map/ppermute | solution.py:217
  14.0 8.1 %collective-permute-start = (f32[3,512]{1,0:T(4,128)S(1)}, f32[3,512]{1,0:T(4,128)S(1)}, u32[]{:S(2)}, u32[]{:S(2)}) collective-permute-start(f32[3,512]{1,0:T(4,128)S(1)} %get-tuple-element.32.pos), channel_id=1, source_target_pairs={{10,0},{11,1},{8,2},{9,3},{2,8},{3,9},{0,10},{1,11},{14,4},{15,5},... | collective-permute-start | bytes 18440 | tf_op jit(solution)/shard_map/ppermute | solution.py:248
  17.2 8.2 %collective-permute-start.4 = (bf16[128,512]{1,0:T(8,128)(2,1)S(1)}, bf16[128,512]{1,0:T(8,128)(2,1)S(1)}, u32[]{:S(2)}, u32[]{:S(2)}) collective-permute-start(bf16[128,512]{1,0:T(8,128)(2,1)S(1)} %get-tuple-element.52), channel_id=1, source_target_pairs={{0,2},{4,14},{1,3},{5,15},{2,8},{6,4},{3,9},{7,5},{8,10},{12,6},{9... | collective-permute-start | bytes 393224 | tf_op jit(solution)/shard_map/ppermute | solution.py:260
  17.3 9.1 %collective-permute-start.7 = (bf16[128,512]{1,0:T(8,128)(2,1)S(1)}, bf16[128,512]{1,0:T(8,128)(2,1)S(1)}, u32[]{:S(2)}, u32[]{:S(2)}) collective-permute-start(bf16[128,512]{1,0:T(8,128)(2,1)S(1)} %get-tuple-element.51), channel_id=1, source_target_pairs={{0,11},{4,5},{1,0},{5,6},{2,1},{6,7},{3,2},{7,12},{8,3},{12,13},{9... | collective-permute-start | bytes 393224 | tf_op jit(solution)/shard_map/ppermute | solution.py:260
  22.2 6.2 %collective-permute-start.6 = (bf16[128,512]{1,0:T(8,128)(2,1)S(1)}, bf16[128,512]{1,0:T(8,128)(2,1)S(1)}, u32[]{:S(2)}, u32[]{:S(2)}) collective-permute-start(bf16[128,512]{1,0:T(8,128)(2,1)S(1)} %get-tuple-element.52), channel_id=1, source_target_pairs={{0,1},{4,15},{1,2},{5,4},{2,3},{6,5},{3,8},{7,6},{8,9},{12,7},{9,1... | collective-permute-start | bytes 393224 | tf_op jit(solution)/shard_map/ppermute | solution.py:260
  28.7 2.0 %collective-permute-start.8 = (bf16[16,32,512]{2,1,0:T(8,128)(2,1)S(1)}, bf16[16,32,512]{2,1,0:T(8,128)(2,1)S(1)}, u32[]{:S(2)}, u32[]{:S(2)}) collective-permute-start(bf16[16,32,512]{2,1,0:T(8,128)(2,1)S(1)} %shard_map.81), channel_id=1, source_target_pairs={{0,4},{4,0},{1,5},{5,1},{2,6},{6,2},{3,7},{7,3},{8,12},{12,8},{9,1... | collective-permute-start | bytes 1572872 | tf_op jit(solution)/shard_map/ppermute | solution.py:220
  29.1 19.4 %copy-start = (bf16[16,256]{1,0:T(8,128)(2,1)S(1)}, bf16[16,256]{1,0:T(8,128)(2,1)}, u32[]{:S(2)}) copy-start(bf16[16,256]{1,0:T(8,128)(2,1)} %refs_1_.1) | copy-start | bytes 24580
  62.5 1.9 %collective-permute-start.9 = (bf16[16,32,512]{2,1,0:T(8,128)(2,1)S(1)}, bf16[16,32,512]{2,1,0:T(8,128)(2,1)S(1)}, u32[]{:S(2)}, u32[]{:S(2)}) collective-permute-start(bf16[16,32,512]{2,1,0:T(8,128)(2,1)S(1)} %all_to_all.16.stacked), channel_id=1, source_target_pairs={{0,4},{4,0},{1,5},{5,1},{2,6},{6,2},{3,7},{7,3},{8,12},{12,8},{9,1... | collective-permute-start | bytes 1572872 | tf_op jit(solution)/shard_map/ppermute | solution.py:220

commit v3 on v1

--- a/solution.py
+++ b/solution.py
@@ -100,16 +100,17 @@
 def early_kernel(cs, *refs):
     pieces, out = refs[:-1], refs[-1]
     rows = cs[...].reshape(-1, cs.shape[4])
-    n = rows.shape[1] // 2
-    rows = jnp.concatenate([rows[:, :n], rows[:, n + LANES :]], 1)
-    part = jnp.dot(rows, joined(pieces), preferred_element_type=F32)
+    n, m = 3 * LANES, rows.shape[1] - 3 * LANES
+    parts = [rows[:, :n], rows[:, n + LANES : m], rows[:, m + LANES :]]
+    part = jnp.dot(jnp.concatenate(parts, 1), joined(pieces), preferred_element_type=F32)
     out[...] = part.reshape(out.shape)
 
 
-def late_kernel(dc, cs, early, block, out):
+def late_kernel(dc, cs, early, ahead, behind, out):
     rows = cs[dc].reshape(-1, cs.shape[4])
-    n = rows.shape[1] // 2
-    part = jnp.dot(rows[:, n : n + LANES], block[...], preferred_element_type=F32)
+    n, m = 3 * LANES, rows.shape[1] - 3 * LANES
+    rows = jnp.concatenate([rows[:, n : n + LANES], rows[:, m : m + LANES]], 1)
+    part = jnp.dot(rows, joined([ahead, behind]), preferred_element_type=F32)
     out[...] = (part.reshape(out.shape) + early[dc]).astype(out.dtype)
 
 
@@ -241,7 +242,6 @@
         2,
         scratch=[pltpu.VMEM((n_xy, LANES, 8), F32)],
     )(pos_near, wv_near)
-    own, trig, pos_near = lax.optimization_barrier((own, trig, pos_near))
     pieces[1], pieces[7] = along_z(own, 1), along_z(own, -1)
     turns = [2 if i % (n_z // 2) < n_z // 4 else -2 for i in range(n_z)]
     pos_far = lax.ppermute(pos_near, Z, [((i - turns[i]) % n_z, i) for i in range(n_z)])
@@ -256,11 +256,12 @@
     pairs = [(at(z, c), at((z + 2 - 4 * c) % n_z, c)) for z in range(n_z) for c in range(2)]
     pieces[4] = lax.ppermute(onward, ("zh", "core", "zl"), pairs)
     pieces[3], pieces[5] = along_z(ahead, 1), along_z(behind, -1)
+    late_blocks = [pieces[3], pieces[5]]
     blocks = [pieces[k] for k in range(n_z)]
     cs = call(trig_far_kernel, cs_shape, 3, aliases={2: 0})(pos_far, trig[2], trig[0])
     kvrel = trig[1]
 
-    near_blocks = [blocks[k] for k in range(n_z) if k != n_z // 2]
+    near_blocks = [blocks[k] for k in range(n_z) if k not in (3, n_z - 3)]
     early = call(
         early_kernel, shape((2, n_xy, 32, 2 * width), F32), 1 + len(near_blocks)
     )(cs, *near_blocks)
@@ -269,8 +270,8 @@
         return call(
             lambda *refs: late_kernel(dc, *refs),
             shape((n_xy, 32, 2 * width), dtype),
-            3,
-        )(cs, early, pieces[4])
+            2 + len(late_blocks),
+        )(cs, early, *late_blocks)
 
     theirs = across(spectra(1, BF16))
     mine = (spectra(0, F32) + theirs.astype(F32)).astype(BF16)

time: 90 us -> 88.2 us (0.980)
  waiting for transfers between devices: 9.04 us -> 7.95 us
    ppermute x6, waiting for transfers between devices: 4.64 us -> 2.81 us  [along_z(): return lax.ppermute(a, Z, [(i, (i + k) % n_z) for i in range(n_z)])]
  transfers between devices with their start and end apart: 10 -> 10, of which waited for: 7 -> 6; matrix products, arithmetic and copies ran while one was open for 0% -> 0% of each run, Pallas kernels for 8% -> 7%
where the time goes in v3:
time: 88.2 us; the launch traced here: 86.9 us
  blocking collectives  52.5 us (60%)
  starting transfers between devices  15.6 us (18%)
  Pallas kernels  9.86 us (11%)
  waiting for transfers between devices  7.95 us (9%)
    all_to_all x1, blocking collectives, body(): lax.all_to_all(parts, Z, 0, 0, tiled=True)  21 us
    all_to_all x1, blocking collectives, body(): arrived = lax.all_to_all(mine, XY, 0, 0, tiled=True)  17.6 us
    all_to_all x1, blocking collectives, body(): near = lax.all_to_all(copies, XY, 0, 0, tiled=True)  13.9 us
    ppermute x6, starting transfers between devices, along_z(): return lax.ppermute(a, Z, [(i, (i + k) % n_z) for i in range(n_z)])  12.9 us
    ppermute x6, waiting for transfers between devices, along_z(): return lax.ppermute(a, Z, [(i, (i + k) % n_z) for i in range(n_z)])  2.81 us
    ppermute x1, starting transfers between devices, body(): lax.ppermute(pos_near, Z, [((i - turns[i]) % n_z, i) for i in range(n_z)])  2.47 us
    ppermute x2, waiting for transfers between devices, across(): return lax.ppermute(a, 'core', [(0, 1), (1, 0)])  2.3 us
    pallas_call x1, Pallas kernels, body(): call(trig_near_kernel, (cs_shape, shape((n_rows, 16), BF16), shape((n_row...  2.26 us
  transfers between devices with their start and end apart: 10, of which 6 were waited for; matrix products, arithmetic and copies ran while one was open for 0% of the time, Pallas kernels for 7%

profile of v3, /device:TPU:8, one launch (start us, length us, event | category | flops | bytes accessed | tf_op | source)
XLA Modules:
  0.0 86.9 jit_solution(6019470786901291819)
XLA Ops:
  0.6 1.0 %shard_map.76 = (bf16[128,512]{1,0:T(8,128)(2,1)S(1)}, f32[3,512]{1,0:T(4,128)S(1)}, f32[3,4096]{1,0:T(4,128)S(1)}) custom-call(bf16[128,256]{1,0:T(8,128)(2,1)} %cot.1, bf16[128,256]{1,0:T(8,128)(2,1)} %feat.1, f32[3,512]{1,0:T(4,128)} %pos.1, f32[3,4096]{1,0:T(4,128)} %wv.1), custom_call_target="tpu_custom_call" | custom-call | tf_op jit(solution)/shard_map/pallas_call | solution.py:224
  1.6 6.4 %collective-permute-start.2 = (bf16[128,512]{1,0:T(8,128)(2,1)S(1)}, bf16[128,512]{1,0:T(8,128)(2,1)S(1)}, u32[]{:S(2)}, u32[]{:S(2)}) collective-permute-start(bf16[128,512]{1,0:T(8,128)(2,1)S(1)} %get-tuple-element.19.refs_0_), channel_id=1, source_target_pairs={{0,10},{1,11},{2,0},{3,1},{8,2},{9,3},{10,8},{11,9},{4,14},{5,15},... | collective-permute-start | bytes 393224 | tf_op jit(solution)/shard_map/ppermute | solution.py:217
  8.0 0.0 collective-permute-start.1
  8.0 3.7 %collective-permute-start.5 = (bf16[128,512]{1,0:T(8,128)(2,1)S(1)}, bf16[128,512]{1,0:T(8,128)(2,1)S(1)}, u32[]{:S(2)}, u32[]{:S(2)}) collective-permute-start(bf16[128,512]{1,0:T(8,128)(2,1)S(1)} %get-tuple-element.19.refs_0_), channel_id=1, source_target_pairs={{0,11},{1,0},{2,1},{3,2},{8,3},{9,8},{10,9},{11,10},{4,15},{5,4},{... | collective-permute-start | bytes 393224 | tf_op jit(solution)/shard_map/ppermute | solution.py:217
  11.7 0.0 collective-permute-start.3
  11.7 2.5 %collective-permute-start = (f32[3,512]{1,0:T(4,128)S(1)}, f32[3,512]{1,0:T(4,128)S(1)}, u32[]{:S(2)}, u32[]{:S(2)}) collective-permute-start(f32[3,512]{1,0:T(4,128)S(1)} %get-tuple-element.18.pos), channel_id=1, source_target_pairs={{10,0},{11,1},{8,2},{9,3},{2,8},{3,9},{0,10},{1,11},{14,4},{15,5},... | collective-permute-start | bytes 18440 | tf_op jit(solution)/shard_map/ppermute | solution.py:247
  14.1 2.3 %shard_map.77 = (bf16[2,16,2,16,1024]{4,3,2,1,0:T(8,128)(2,1)S(1)}, bf16[512,16]{1,0:T(8,128)(2,1)S(1)}, f32[512,8]{1,0:T(8,128)S(1)}) custom-call(f32[3,512]{1,0:T(4,128)S(1)} %get-tuple-element.18.pos, f32[3,4096]{1,0:T(4,128)S(1)} %get-tuple-element.20.wv), custom_call_target="tpu_custom_call" | custom-call | tf_op jit(solution)/shard_map/pallas_call | solution.py:239
  16.4 0.0 collective-permute-done.2.refs_4_.refs_6_
  16.4 1.9 %collective-permute-done.1.refs_2_ = bf16[128,512]{1,0:T(8,128)(2,1)S(1)} collective-permute-done((bf16[128,512]{1,0:T(8,128)(2,1)S(1)}, bf16[128,512]{1,0:T(8,128)(2,1)S(1)}, u32[]{:S(2)}, u32[]{:S(2)}) %collective-permute-start.1) | collective-permute-done | bytes 131104 | tf_op jit(solution)/shard_map/ppermute | solution.py:217
  18.3 0.1 collective-permute-start.4
  18.4 1.1 %collective-permute-start.6 = (bf16[128,512]{1,0:T(8,128)(2,1)S(1)}, bf16[128,512]{1,0:T(8,128)(2,1)S(1)}, u32[]{:S(2)}, u32[]{:S(2)}) collective-permute-start(bf16[128,512]{1,0:T(8,128)(2,1)S(1)} %collective-permute-done.1.refs_2_), channel_id=1, source_target_pairs={{0,1},{1,2},{2,3},{3,8},{8,9},{9,10},{10,11},{11,0},{4,5},{5,6},{6... | collective-permute-start | bytes 393224 | tf_op jit(solution)/shard_map/ppermute | solution.py:217
  19.5 0.8 collective-permute-done.pos
  20.3 1.8 %collective-permute-start.7 = (bf16[128,512]{1,0:T(8,128)(2,1)S(1)}, bf16[128,512]{1,0:T(8,128)(2,1)S(1)}, u32[]{:S(2)}, u32[]{:S(2)}) collective-permute-start(bf16[128,512]{1,0:T(8,128)(2,1)S(1)} %collective-permute-done.2.refs_4_.refs_6_), channel_id=1, source_target_pairs={{0,11},{1,0},{2,1},{3,2},{8,3},{9,8},{10,9},{11,10},{4,15},{5,4},{... | collective-permute-start | bytes 393224 | tf_op jit(solution)/shard_map/ppermute | solution.py:217
  22.1 1.8 %shard_map.78.cs.refs_0_ = bf16[2,16,2,16,1024]{4,3,2,1,0:T(8,128)(2,1)S(1)} custom-call(f32[3,512]{1,0:T(4,128)S(1)} %collective-permute-done.pos, f32[512,8]{1,0:T(8,128)S(1)} %get-tuple-element.24.kcols, bf16[2,16,2,16,1024]{4,3,2,1,0:T(8,128)(2,1)S(1)} %get-tuple-element.25._), custom_call_target="tpu_custom_call", output_to_operand_aliasing={{}: (2, {})} | custom-call | tf_op jit(solution)/shard_map/pallas_call | solution.py:261
  23.9 0.0 collective-permute-done.5.refs_5_.refs_7_
  23.9 0.0 collective-permute-done.3.refs_1_
  23.9 2.0 %collective-permute-done.4.refs_3_.refs_4_ = bf16[128,512]{1,0:T(8,128)(2,1)S(1)} collective-permute-done((bf16[128,512]{1,0:T(8,128)(2,1)S(1)}, bf16[128,512]{1,0:T(8,128)(2,1)S(1)}, u32[]{:S(2)}, u32[]{:S(2)}) %collective-permute-start.4) | collective-permute-done | bytes 131104 | tf_op jit(solution)/shard_map/ppermute | solution.py:257
  25.9 1.0 %shard_map.79.refs_1_ = f32[2,16,32,512]{3,2,1,0:T(8,128)S(1)} custom-call(bf16[2,16,2,16,1024]{4,3,2,1,0:T(8,128)(2,1)S(1)} %shard_map.78.cs.refs_0_, bf16[128,512]{1,0:T(8,128)(2,1)S(1)} %get-tuple-element.19.refs_0_, bf16[128,512]{1,0:T(8,128)(2,1)S(1)} %collective-permute-done.3.refs_1_, bf16[128,512]{1,0:T(8,128)(2,1)S(1)} %collective-permute-done.1.refs_2_, ...), custom_call_target="tpu_custom_call" | custom-call | tf_op jit(solution)/shard_map/pallas_call | solution.py:265
  26.9 0.9 %collective-permute-done.6.refs_2_.refs_3_ = bf16[128,512]{1,0:T(8,128)(2,1)S(1)} collective-permute-done((bf16[128,512]{1,0:T(8,128)(2,1)S(1)}, bf16[128,512]{1,0:T(8,128)(2,1)S(1)}, u32[]{:S(2)}, u32[]{:S(2)}) %collective-permute-start.6) | collective-permute-done | bytes 131104 | tf_op jit(solution)/shard_map/ppermute | solution.py:217
  27.8 0.0 collective-permute-done.7.refs_3_.refs_5_
  27.8 0.3 shard_map.81
  28.1 0.1 collective-permute-start.8
  28.2 0.3 shard_map.80
  28.5 0.0 copy-start
  28.5 1.6 %collective-permute-done.8 = bf16[16,32,512]{2,1,0:T(8,128)(2,1)S(1)} collective-permute-done((bf16[16,32,512]{2,1,0:T(8,128)(2,1)S(1)}, bf16[16,32,512]{2,1,0:T(8,128)(2,1)S(1)}, u32[]{:S(2)}, u32[]{:S(2)}) %collective-permute-start.8) | collective-permute-done | bytes 524320 | tf_op jit(solution)/shard_map/ppermute | solution.py:220
  30.1 0.2 add_convert_fusion
  30.3 17.6 %all_to_all.15.refs_0_ = bf16[16,32,512]{2,1,0:T(8,128)(2,1)S(1)} all-to-all(bf16[16,32,512]{2,1,0:T(8,128)(2,1)S(1)} %add_convert_fusion), channel_id=1, replica_groups=mesh['x'=4,'y'=4,'zh'=2,'core'=2,'zl'=4] {'x','y'}, dimensions={0} | all-to-all | bytes 1048576 | tf_op jit(solution)/shard_map/all_to_all | solution.py:278
  47.9 0.0 copy-done
  47.9 0.1 shard_map.82
  48.0 13.9 %all_to_all.16.stacked = bf16[16,32,512]{2,1,0:T(8,128)(2,1)S(1)} all-to-all(bf16[16,32,512]{2,1,0:T(8,128)(2,1)S(1)} %get-tuple-element.29), channel_id=1, replica_groups=mesh['x'=4,'y'=4,'zh'=2,'core'=2,'zl'=4] {'x','y'}, dimensions={0} | all-to-all | bytes 1048576 | tf_op jit(solution)/shard_map/all_to_all | solution.py:284
  61.9 0.0 collective-permute-start.9
  61.9 1.2 %shard_map.83 = (f32[256,1024]{1,0:T(8,128)S(1)}, f32[8,1024]{1,0:T(8,128)S(1)}) custom-call(bf16[2,16,2,16,1024]{4,3,2,1,0:T(8,128)(2,1)S(1)} %shard_map.78.cs.refs_0_, bf16[512,16]{1,0:T(8,128)(2,1)S(1)} %get-tuple-element.26.kvrel, bf16[16,32,512]{2,1,0:T(8,128)(2,1)S(1)} %all_to_all.16.stacked, bf16[128,512]{1,0:T(8,128)(2,1)S(1)} %get-tuple-element.19.refs_0_, ...), custom_call_target="tpu_custom_call" | custom-call | tf_op jit(solution)/shard_map/pallas_call | solution.py:286
  63.1 0.7 collective-permute-done.9.stacked
  63.8 1.2 %shard_map.84 = bf16[8,264,128]{2,1,0:T(8,128)(2,1)S(1)} custom-call(bf16[2,16,2,16,1024]{4,3,2,1,0:T(8,128)(2,1)S(1)} %shard_map.78.cs.refs_0_, bf16[512,16]{1,0:T(8,128)(2,1)S(1)} %get-tuple-element.26.kvrel, bf16[16,32,512]{2,1,0:T(8,128)(2,1)S(1)} %collective-permute-done.9.stacked, f32[256,1024]{1,0:T(8,128)S(1)} %get-tuple-element.30.gf_in, ...), custom_call_target="tpu_custom_call" | custom-call | tf_op jit(solution)/shard_map/pallas_call | solution.py:291
  65.1 21.0 %all_to_all.17.refs_0_ = bf16[8,264,128]{2,1,0:T(8,128)(2,1)S(1)} all-to-all(bf16[8,264,128]{2,1,0:T(8,128)(2,1)S(1)} %shard_map.84), channel_id=1, replica_groups=mesh['x'=4,'y'=4,'zh'=2,'core'=2,'zl'=4] {'zh','zl'}, dimensions={0} | all-to-all | bytes 1081344 | tf_op jit(solution)/shard_map/all_to_all | solution.py:302
  86.1 0.8 shard_map.85
  (1 shorter events, 0.0 us)
Async XLA Ops:
  1.6 14.8 %collective-permute-start.2 = (bf16[128,512]{1,0:T(8,128)(2,1)S(1)}, bf16[128,512]{1,0:T(8,128)(2,1)S(1)}, u32[]{:S(2)}, u32[]{:S(2)}) collective-permute-start(bf16[128,512]{1,0:T(8,128)(2,1)S(1)} %get-tuple-element.19.refs_0_), channel_id=1, source_target_pairs={{0,10},{1,11},{2,0},{3,1},{8,2},{9,3},{10,8},{11,9},{4,14},{5,15},... | collective-permute-start | bytes 393224 | tf_op jit(solution)/shard_map/ppermute | solution.py:217
  8.0 10.3 %collective-permute-start.1 = (bf16[128,512]{1,0:T(8,128)(2,1)S(1)}, bf16[128,512]{1,0:T(8,128)(2,1)S(1)}, u32[]{:S(2)}, u32[]{:S(2)}) collective-permute-start(bf16[128,512]{1,0:T(8,128)(2,1)S(1)} %get-tuple-element.19.refs_0_), channel_id=1, source_target_pairs={{0,2},{1,3},{2,8},{3,9},{8,10},{9,11},{10,0},{11,1},{4,6},{5,7},{6... | collective-permute-start | bytes 393224 | tf_op jit(solution)/shard_map/ppermute | solution.py:217
  8.0 15.9 %collective-permute-start.5 = (bf16[128,512]{1,0:T(8,128)(2,1)S(1)}, bf16[128,512]{1,0:T(8,128)(2,1)S(1)}, u32[]{:S(2)}, u32[]{:S(2)}) collective-permute-start(bf16[128,512]{1,0:T(8,128)(2,1)S(1)} %get-tuple-element.19.refs_0_), channel_id=1, source_target_pairs={{0,11},{1,0},{2,1},{3,2},{8,3},{9,8},{10,9},{11,10},{4,15},{5,4},{... | collective-permute-start | bytes 393224 | tf_op jit(solution)/shard_map/ppermute | solution.py:217
  11.7 12.2 %collective-permute-start.3 = (bf16[128,512]{1,0:T(8,128)(2,1)S(1)}, bf16[128,512]{1,0:T(8,128)(2,1)S(1)}, u32[]{:S(2)}, u32[]{:S(2)}) collective-permute-start(bf16[128,512]{1,0:T(8,128)(2,1)S(1)} %get-tuple-element.19.refs_0_), channel_id=1, source_target_pairs={{0,1},{1,2},{2,3},{3,8},{8,9},{9,10},{10,11},{11,0},{4,5},{5,6},{6... | collective-permute-start | bytes 393224 | tf_op jit(solution)/shard_map/ppermute | solution.py:217
  11.7 8.6 %collective-permute-start = (f32[3,512]{1,0:T(4,128)S(1)}, f32[3,512]{1,0:T(4,128)S(1)}, u32[]{:S(2)}, u32[]{:S(2)}) collective-permute-start(f32[3,512]{1,0:T(4,128)S(1)} %get-tuple-element.18.pos), channel_id=1, source_target_pairs={{10,0},{11,1},{8,2},{9,3},{2,8},{3,9},{0,10},{1,11},{14,4},{15,5},... | collective-permute-start | bytes 18440 | tf_op jit(solution)/shard_map/ppermute | solution.py:247
  18.3 7.6 %collective-permute-start.4 = (bf16[128,512]{1,0:T(8,128)(2,1)S(1)}, bf16[128,512]{1,0:T(8,128)(2,1)S(1)}, u32[]{:S(2)}, u32[]{:S(2)}) collective-permute-start(bf16[128,512]{1,0:T(8,128)(2,1)S(1)} %broadcast_select_fusion), channel_id=1, source_target_pairs={{0,2},{4,14},{1,3},{5,15},{2,8},{6,4},{3,9},{7,5},{8,10},{12,6},{9... | collective-permute-start | bytes 393224 | tf_op jit(solution)/shard_map/ppermute | solution.py:257
  18.4 9.4 %collective-permute-start.6 = (bf16[128,512]{1,0:T(8,128)(2,1)S(1)}, bf16[128,512]{1,0:T(8,128)(2,1)S(1)}, u32[]{:S(2)}, u32[]{:S(2)}) collective-permute-start(bf16[128,512]{1,0:T(8,128)(2,1)S(1)} %collective-permute-done.1.refs_2_), channel_id=1, source_target_pairs={{0,1},{1,2},{2,3},{3,8},{8,9},{9,10},{10,11},{11,0},{4,5},{5,6},{6... | collective-permute-start | bytes 393224 | tf_op jit(solution)/shard_map/ppermute | solution.py:217
  20.3 7.5 %collective-permute-start.7 = (bf16[128,512]{1,0:T(8,128)(2,1)S(1)}, bf16[128,512]{1,0:T(8,128)(2,1)S(1)}, u32[]{:S(2)}, u32[]{:S(2)}) collective-permute-start(bf16[128,512]{1,0:T(8,128)(2,1)S(1)} %collective-permute-done.2.refs_4_.refs_6_), channel_id=1, source_target_pairs={{0,11},{1,0},{2,1},{3,2},{8,3},{9,8},{10,9},{11,10},{4,15},{5,4},{... | collective-permute-start | bytes 393224 | tf_op jit(solution)/shard_map/ppermute | solution.py:217
  28.1 2.0 %collective-permute-start.8 = (bf16[16,32,512]{2,1,0:T(8,128)(2,1)S(1)}, bf16[16,32,512]{2,1,0:T(8,128)(2,1)S(1)}, u32[]{:S(2)}, u32[]{:S(2)}) collective-permute-start(bf16[16,32,512]{2,1,0:T(8,128)(2,1)S(1)} %shard_map.81), channel_id=1, source_target_pairs={{0,4},{4,0},{1,5},{5,1},{2,6},{6,2},{3,7},{7,3},{8,12},{12,8},{9,1... | collective-permute-start | bytes 1572872 | tf_op jit(solution)/shard_map/ppermute | solution.py:220
  28.5 19.4 %copy-start = (bf16[16,256]{1,0:T(8,128)(2,1)S(1)}, bf16[16,256]{1,0:T(8,128)(2,1)}, u32[]{:S(2)}) copy-start(bf16[16,256]{1,0:T(8,128)(2,1)} %refs_1_.1) | copy-start | bytes 24580
  61.9 1.9 %collective-permute-start.9 = (bf16[16,32,512]{2,1,0:T(8,128)(2,1)S(1)}, bf16[16,32,512]{2,1,0:T(8,128)(2,1)S(1)}, u32[]{:S(2)}, u32[]{:S(2)}) collective-permute-start(bf16[16,32,512]{2,1,0:T(8,128)(2,1)S(1)} %all_to_all.16.stacked), channel_id=1, source_target_pairs={{0,4},{4,0},{1,5},{5,1},{2,6},{6,2},{3,7},{7,3},{8,12},{12,8},{9,1... | collective-permute-start | bytes 1572872 | tf_op jit(solution)/shard_map/ppermute | solution.py:220
